TPU v7x, 256 devices: a whole 4x4x8 slice. The times are simulated.
256 devices in a mesh: dp: 4 (over x), seq: 16 (over z, core), tensor: 4 (over y).
Axes of the slice: x: 4, y: 4, z: 8, core: 2. Of those that a mesh axis runs over, the one named last changes fastest.
Arguments:
- feature_in: bfloat16 [16, 2048, 512], P('dp', 'seq', 'tensor'), may hold values from -6 to 6
- conv_weight: bfloat16 [2, 512, 512], P(None, 'tensor'), may hold values from -0.1875 to 0.1875
- proj_weight: bfloat16 [512, 1920], P(None, 'tensor'), may hold values from -0.25 to 0.25
- mask_embed: bfloat16 [1920], P('tensor'), may hold values from -5 to 5
- pos_weight: bfloat16 [128, 16, 120, 120], P(('dp', 'seq'), 'tensor'), may hold values from -0.046875 to 0.046875
- final_weight: bfloat16 [1920, 1024], P('tensor'), may hold values from -0.125 to 0.125
- codebook: bfloat16 [2, 320, 512], replicated, may hold values from -6 to 6
- quant_weight: bfloat16 [1024, 1024], replicated, may hold values from -0.1875 to 0.1875
- mask_starts: int32 [16, 66], P('dp'), may hold values from 0 to 1014
- code_choice: int32 [16, 1024, 2], P(('dp', 'tensor'), 'seq'), may hold values from 0 to 319
- negative_ids: int32 [16, 1024, 100], P(('dp', 'tensor'), 'seq'), may hold values from 0 to 1023, as said below
Outputs:
- frame_loss: float32 [16, 1024], P(('dp', 'tensor'), 'seq')
Inputs may be any that keep to these rules, and one draw needn't show every extreme that they name: `negative_ids`: each entry names a frame of the same utterance other than the frame itself.
All inputs are finite; a program needn't handle non-finite values.
Results may differ from a plain program's by a relative error of at most 0.00065.
Values may be sent and summed in bfloat16 or wider, within the bound.
A program may use at most 128 MiB of HBM per device.

v0:
```python
import jax
import jax.numpy as jnp
from jax import lax
from jax.sharding import PartitionSpec as P

KERNEL = 128
MASK_LEN = 10


ln_eps = 1e-05
norm_eps = 1e-06
logit_temp = 0.1


def extended(block, sides, width):
    for axis, dim in sides:
        count = lax.axis_size(axis)
        forward = [(i, i + 1) for i in range(count - 1)]
        backward = [(target, source) for source, target in forward]
        low = lax.ppermute(
            lax.slice_in_dim(block, block.shape[dim] - width, None, axis=dim), axis, forward
        )
        high = lax.ppermute(lax.slice_in_dim(block, 0, width, axis=dim), axis, backward)
        block = jnp.concatenate([low, block, high], axis=dim)
    return block


def make_targets(code_block, codebook, quant_weight):
    entries = codebook.shape[1]
    choices_row = jnp.arange(entries, dtype=jnp.int32)
    pieces = []
    for qgroup in range(codebook.shape[0]):
        onehot = (code_block[..., qgroup, None] == choices_row).astype(jnp.bfloat16)
        pieces.append(
            jnp.dot(onehot, codebook[qgroup], preferred_element_type=jnp.float32).astype(
                jnp.bfloat16
            )
        )
    codevec = jnp.concatenate(pieces, axis=-1)
    return jnp.dot(codevec, quant_weight, preferred_element_type=jnp.float32).astype(jnp.bfloat16)


def utterance_loss(context, own_targets, all_targets, neg_ids, is_masked):
    scores = jnp.einsum("fc,nc->fn", context, all_targets, preferred_element_type=jnp.float32)
    ctx_norm = jnp.einsum("fc,fc->f", context, context, preferred_element_type=jnp.float32)
    own_norm = jnp.einsum("fc,fc->f", own_targets, own_targets, preferred_element_type=jnp.float32)
    tgt_norm = jnp.einsum("nc,nc->n", all_targets, all_targets, preferred_element_type=jnp.float32)
    pos_dot = jnp.einsum("fc,fc->f", context, own_targets, preferred_element_type=jnp.float32)
    neg_dot = jnp.take_along_axis(scores, neg_ids, axis=1)
    neg_norm = tgt_norm[neg_ids]
    positive = pos_dot * lax.rsqrt((ctx_norm + norm_eps) * (own_norm + norm_eps)) / logit_temp
    negative = (
        neg_dot * lax.rsqrt((ctx_norm[:, None] + norm_eps) * (neg_norm + norm_eps)) / logit_temp
    )
    frame_loss = jnp.log(jnp.exp(positive) + jnp.sum(jnp.exp(negative), axis=-1)) - positive
    return jnp.where(is_masked, frame_loss, jnp.zeros_like(frame_loss))


def tap_sum(windows, running, tap_block, frames):
    count = tap_block.shape[0]
    joined_taps = max((d for d in range(1, 17) if count % d == 0))
    group_count, inner, outer = (tap_block.shape[1], tap_block.shape[2], tap_block.shape[3])

    def add_block(step, partial_value):
        base = step * joined_taps
        slabs = [
            lax.dynamic_slice_in_dim(windows, base + offset, frames, 1)
            for offset in range(joined_taps)
        ]
        joined = jnp.concatenate(slabs, axis=-1)
        taps = lax.dynamic_slice_in_dim(tap_block, base, joined_taps, 0)
        taps = jnp.transpose(taps, (1, 0, 2, 3)).reshape(group_count, joined_taps * inner, outer)
        return partial_value + jnp.einsum(
            "ufgi,gio->ufgo", joined, taps, preferred_element_type=jnp.float32
        )

    return lax.fori_loop(0, count // joined_taps, add_block, running)


def on_device(
    feature_in,
    conv_weight,
    proj_weight,
    mask_embed,
    pos_weight,
    final_weight,
    codebook,
    quant_weight,
    mask_starts,
    code_choice,
    negative_ids,
):
    utt_count, sample_rows, channels = feature_in.shape
    frames = sample_rows // 2
    frame_pairs = feature_in.reshape(utt_count, frames, 2 * channels)
    conv_term = jnp.dot(
        frame_pairs,
        conv_weight.reshape(2 * channels, conv_weight.shape[2]),
        preferred_element_type=jnp.float32,
    )
    summed = lax.psum(conv_term, "tensor")
    row_mean = jnp.mean(summed, axis=-1, keepdims=True)
    row_square = jnp.mean(summed * summed, axis=-1, keepdims=True)
    normed = (summed - row_mean) * lax.rsqrt(row_square - row_mean * row_mean + ln_eps)
    features = jax.nn.gelu(normed, approximate=False).astype(jnp.bfloat16)
    projected = jnp.dot(features, proj_weight, preferred_element_type=jnp.float32).astype(
        jnp.bfloat16
    )
    positions = (lax.axis_index("seq") * frames + jnp.arange(frames, dtype=jnp.int32))[
        None, :, None
    ]
    starts = mask_starts[:, None, :]
    masked = jnp.any((positions >= starts) & (positions < starts + MASK_LEN), axis=-1)
    hidden = jnp.where(masked[..., None], mask_embed[None, None, :], projected)
    padded = extended(hidden, (("seq", 1),), KERNEL // 2)
    group_count = pos_weight.shape[1]
    inner = pos_weight.shape[2]
    outer = pos_weight.shape[3]
    windows = padded.reshape(utt_count, padded.shape[1], group_count, inner)
    initial = jnp.zeros((utt_count, frames, group_count, outer), jnp.float32)
    conv_out = tap_sum(
        windows, initial, lax.all_gather(pos_weight, ("dp", "seq"), axis=0, tiled=True), frames
    )
    conv_out = conv_out.reshape(utt_count, frames, group_count * outer)
    mixed = (hidden.astype(jnp.float32) + jax.nn.gelu(conv_out, approximate=False)).astype(
        jnp.bfloat16
    )
    utt_rows = utt_count // lax.axis_size("tensor")
    context = lax.psum_scatter(
        jnp.dot(mixed, final_weight, preferred_element_type=jnp.float32),
        "tensor",
        scatter_dimension=0,
        tiled=True,
    ).astype(jnp.bfloat16)
    own_targets = make_targets(code_choice, codebook, quant_weight)
    all_targets = lax.all_gather(own_targets, "seq", axis=1, tiled=True)
    is_masked = lax.dynamic_slice_in_dim(masked, lax.axis_index("tensor") * utt_rows, utt_rows, 0)
    return jax.vmap(utterance_loss)(context, own_targets, all_targets, negative_ids, is_masked)


def solution(mesh):
    return jax.shard_map(
        on_device,
        mesh=mesh,
        in_specs=(
            P("dp", "seq", "tensor"),
            P(None, "tensor", None),
            P(None, "tensor"),
            P("tensor"),
            P(("dp", "seq"), "tensor", None, None),
            P("tensor", None),
            P(),
            P(),
            P("dp", None),
            P(("dp", "tensor"), "seq", None),
            P(("dp", "tensor"), "seq", None),
        ),
        out_specs=P(("dp", "tensor"), "seq"),
        check_vma=False,
    )
```

profile of v0, /device:TPU:1, one launch (start us, length us, event | category | flops | bytes accessed | tf_op | source)
XLA Modules:
  0.0 506.4 jit_solution(2708013920155017598)
XLA Ops:
  12.7 48.5 %all-reduce.2.cloned.1.call-done = f32[4,64,512]{2,1,0:T(8,128)} async-done(((f32[4,64,512]{2,1,0:T(8,128)}), f32[4,64,512]{2,1,0:T(8,128)}) %all-reduce.2.cloned.1.call-update) | async-done | bytes 524304 | tf_op jit(solution)/shard_map/psum | solution.py:101
  65.0 5.1 %collective-permute-start = (bf16[4,64,480]{2,1,0:T(8,128)(2,1)S(1)}, bf16[4,64,480]{2,1,0:T(8,128)(2,1)S(1)}, u32[]{:S(2)}, u32[]{:S(2)}) collective-permute-start(bf16[4,64,480]{2,1,0:T(8,128)(2,1)S(1)} %fusion.1), channel_id=1, source_target_pairs={{0,4},{4,8},{8,12},{12,16},{16,20},{20,24},{24,28},{28,32},{32,36}... | collective-permute-start | bytes 737288 | tf_op jit(solution)/shard_map/ppermute | solution.py:20
  72.0 6.7 %collective-permute-done = bf16[4,64,480]{2,1,0:T(8,128)(2,1)S(1)} collective-permute-done((bf16[4,64,480]{2,1,0:T(8,128)(2,1)S(1)}, bf16[4,64,480]{2,1,0:T(8,128)(2,1)S(1)}, u32[]{:S(2)}, u32[]{:S(2)}) %collective-permute-start) | collective-permute-done | bytes 245792 | tf_op jit(solution)/shard_map/ppermute | solution.py:20
  86.5 28.4 %all-gather.4.cloned.1.call-done = bf16[128,4,120,120]{3,2,1,0:T(8,128)(2,1)} async-done(((bf16[2,4,120,120]{3,2,1,0:T(8,128)(2,1)}), bf16[128,4,120,120]{3,2,1,0:T(8,128)(2,1)}) %all-gather.4.cloned.1.call-update) | async-done | bytes 14745616 | tf_op jit(solution)/shard_map/all_gather | solution.py:122
  114.9 222.5 %while.16 = (s32[]{:T(128)}, f32[4,64,4,120]{3,1,0,2:T(8,128)}, bf16[128,4,120,120]{3,2,1,0:T(8,128)(2,1)}, bf16[4,192,4,120]{3,1,0,2:T(8,128)(2,1)S(1)}, s32[]{...) while((s32[]{:T(128)}, f32[4,64,4,120]{3,1,0,2:T(8,128)}, ...), condition=%wide.region_5.6_spmd.clone, body=%wide.region_4.5_spmd.clone.sunk | while | flops 472105024 | bytes 34530440 | solution.py:77
  117.9 7.1 %concatenate.26 = bf16[4,64,4,1920]{3,1,0,2:T(8,128)(2,1)} concatenate(bf16[4,64,4,120]{3,1,0,2:T(8,128)(2,1)} %get-tuple-element.238, bf16[4,64,4,120]{3,1,0,2:T(8,128)(2,1)} %get-tuple-element.239, bf16[4,64,4,120]{3,1,0,2:T(8,128)(2,1)} %get-tuple-element.240, bf16[4,64,4,120]{3,1,0,2:T(8,128)(2,1)} %get-tuple-element.241, bf16[4,64,4,120]{3,1,0,2:T(8,128)(2,1)} %get-tuple-element.242, ...), dimensions={3} | concatenate | bytes 7864320 | tf_op jit(solution)/shard_map/while/body/eval_jaxpr/concatenate | solution.py:70
  128.0 4.4 copy.47
  132.5 4.6 reshape.312
  144.8 7.1 %concatenate.26 = bf16[4,64,4,1920]{3,1,0,2:T(8,128)(2,1)} concatenate(bf16[4,64,4,120]{3,1,0,2:T(8,128)(2,1)} %get-tuple-element.238, bf16[4,64,4,120]{3,1,0,2:T(8,128)(2,1)} %get-tuple-element.239, bf16[4,64,4,120]{3,1,0,2:T(8,128)(2,1)} %get-tuple-element.240, bf16[4,64,4,120]{3,1,0,2:T(8,128)(2,1)} %get-tuple-element.241, bf16[4,64,4,120]{3,1,0,2:T(8,128)(2,1)} %get-tuple-element.242, ...), dimensions={3} | concatenate | bytes 7864320 | tf_op jit(solution)/shard_map/while/body/eval_jaxpr/concatenate | solution.py:70
  154.9 4.4 copy.47
  159.4 4.6 reshape.312
  172.7 7.1 %concatenate.26 = bf16[4,64,4,1920]{3,1,0,2:T(8,128)(2,1)} concatenate(bf16[4,64,4,120]{3,1,0,2:T(8,128)(2,1)} %get-tuple-element.238, bf16[4,64,4,120]{3,1,0,2:T(8,128)(2,1)} %get-tuple-element.239, bf16[4,64,4,120]{3,1,0,2:T(8,128)(2,1)} %get-tuple-element.240, bf16[4,64,4,120]{3,1,0,2:T(8,128)(2,1)} %get-tuple-element.241, bf16[4,64,4,120]{3,1,0,2:T(8,128)(2,1)} %get-tuple-element.242, ...), dimensions={3} | concatenate | bytes 7864320 | tf_op jit(solution)/shard_map/while/body/eval_jaxpr/concatenate | solution.py:70
  182.9 4.4 copy.47
  187.3 4.6 reshape.312
  200.7 7.1 %concatenate.26 = bf16[4,64,4,1920]{3,1,0,2:T(8,128)(2,1)} concatenate(bf16[4,64,4,120]{3,1,0,2:T(8,128)(2,1)} %get-tuple-element.238, bf16[4,64,4,120]{3,1,0,2:T(8,128)(2,1)} %get-tuple-element.239, bf16[4,64,4,120]{3,1,0,2:T(8,128)(2,1)} %get-tuple-element.240, bf16[4,64,4,120]{3,1,0,2:T(8,128)(2,1)} %get-tuple-element.241, bf16[4,64,4,120]{3,1,0,2:T(8,128)(2,1)} %get-tuple-element.242, ...), dimensions={3} | concatenate | bytes 7864320 | tf_op jit(solution)/shard_map/while/body/eval_jaxpr/concatenate | solution.py:70
  210.9 4.4 copy.47
  215.3 4.6 reshape.312
  228.6 7.1 %concatenate.26 = bf16[4,64,4,1920]{3,1,0,2:T(8,128)(2,1)} concatenate(bf16[4,64,4,120]{3,1,0,2:T(8,128)(2,1)} %get-tuple-element.238, bf16[4,64,4,120]{3,1,0,2:T(8,128)(2,1)} %get-tuple-element.239, bf16[4,64,4,120]{3,1,0,2:T(8,128)(2,1)} %get-tuple-element.240, bf16[4,64,4,120]{3,1,0,2:T(8,128)(2,1)} %get-tuple-element.241, bf16[4,64,4,120]{3,1,0,2:T(8,128)(2,1)} %get-tuple-element.242, ...), dimensions={3} | concatenate | bytes 7864320 | tf_op jit(solution)/shard_map/while/body/eval_jaxpr/concatenate | solution.py:70
  238.8 4.4 copy.47
  243.2 4.6 reshape.312
  256.5 7.1 %concatenate.26 = bf16[4,64,4,1920]{3,1,0,2:T(8,128)(2,1)} concatenate(bf16[4,64,4,120]{3,1,0,2:T(8,128)(2,1)} %get-tuple-element.238, bf16[4,64,4,120]{3,1,0,2:T(8,128)(2,1)} %get-tuple-element.239, bf16[4,64,4,120]{3,1,0,2:T(8,128)(2,1)} %get-tuple-element.240, bf16[4,64,4,120]{3,1,0,2:T(8,128)(2,1)} %get-tuple-element.241, bf16[4,64,4,120]{3,1,0,2:T(8,128)(2,1)} %get-tuple-element.242, ...), dimensions={3} | concatenate | bytes 7864320 | tf_op jit(solution)/shard_map/while/body/eval_jaxpr/concatenate | solution.py:70
  266.7 4.4 copy.47
  271.2 4.6 reshape.312
  284.5 7.1 %concatenate.26 = bf16[4,64,4,1920]{3,1,0,2:T(8,128)(2,1)} concatenate(bf16[4,64,4,120]{3,1,0,2:T(8,128)(2,1)} %get-tuple-element.238, bf16[4,64,4,120]{3,1,0,2:T(8,128)(2,1)} %get-tuple-element.239, bf16[4,64,4,120]{3,1,0,2:T(8,128)(2,1)} %get-tuple-element.240, bf16[4,64,4,120]{3,1,0,2:T(8,128)(2,1)} %get-tuple-element.241, bf16[4,64,4,120]{3,1,0,2:T(8,128)(2,1)} %get-tuple-element.242, ...), dimensions={3} | concatenate | bytes 7864320 | tf_op jit(solution)/shard_map/while/body/eval_jaxpr/concatenate | solution.py:70
  299.1 4.6 reshape.312
  312.5 7.1 %concatenate.26 = bf16[4,64,4,1920]{3,1,0,2:T(8,128)(2,1)} concatenate(bf16[4,64,4,120]{3,1,0,2:T(8,128)(2,1)} %get-tuple-element.238, bf16[4,64,4,120]{3,1,0,2:T(8,128)(2,1)} %get-tuple-element.239, bf16[4,64,4,120]{3,1,0,2:T(8,128)(2,1)} %get-tuple-element.240, bf16[4,64,4,120]{3,1,0,2:T(8,128)(2,1)} %get-tuple-element.241, bf16[4,64,4,120]{3,1,0,2:T(8,128)(2,1)} %get-tuple-element.242, ...), dimensions={3} | concatenate | bytes 7864320 | tf_op jit(solution)/shard_map/while/body/eval_jaxpr/concatenate | solution.py:70
  322.7 4.4 copy.47
  327.1 4.6 reshape.312
  347.1 19.4 %reduce-scatter.2.cloned.1.call-done = f32[1,64,1024]{2,1,0:T(8,128)} async-done(((f32[4,64,1024]{2,1,0:T(8,128)}), f32[1,64,1024]{2,1,0:T(8,128)}) %reduce-scatter.2.cloned.1.call-update) | async-done | bytes 262160 | tf_op jit(solution)/shard_map/reduce_scatter | solution.py:129
  369.3 41.1 %all-gather.6.cloned.1.call-done = bf16[1024,1024]{1,0:T(8,128)(2,1)} async-done(((bf16[64,1024]{1,0:T(8,128)(2,1)}), bf16[1024,1024]{1,0:T(8,128)(2,1)}) %all-gather.6.cloned.1.call-update) | async-done | bytes 2097168 | tf_op jit(solution)/shard_map/all_gather | solution.py:136
  412.7 48.5 %gather_fusion = f32[6400]{0:T(1024)S(1)} fusion(f32[1,64,1024]{2,1,0:T(8,128)S(1)} %convolution_bitcast_fusion, s32[6400]{0:T(1024)S(1)} %reshape.273), kind=kCustom, calls=%fused_computation | custom fusion | bytes 128000 | tf_op jit(solution)/shard_map/vmap(jit(take_along_axis))/gather | solution.py:49
  463.3 35.1 %gather_fusion.1 = f32[6400]{0:T(1024)S(1)} fusion(f32[1,1024]{1,0:T(1,128)S(1)} %bitcast.82, s32[6400]{0:T(1024)S(1)} %reshape.281), kind=kCustom, calls=%fused_computation.1 | custom fusion | bytes 102400 | tf_op jit(solution)/shard_map/vmap()/gather | solution.py:50
  (94 shorter events, 133.9 us)
Async XLA Ops:
  7.4 359.2 %copy-start = (bf16[1024,1024]{1,0:T(8,128)(2,1)S(1)}, bf16[1024,1024]{1,0:T(8,128)(2,1)}, u32[]{:S(2)}) copy-start(bf16[1024,1024]{1,0:T(8,128)(2,1)} %param.20) | copy-start | bytes 6291460
  7.4 53.8 %all-reduce.2.cloned.1.call-start = ((), (), s32[]{:S(2)}) async-start(), calls=%async_computation.1 | async-start | bytes 1048576 | tf_op jit(solution)/shard_map/psum | solution.py:101
  10.5 104.4 %all-gather.4.cloned.1.call-start = ((), (), s32[]{:S(2)}) async-start(), calls=%async_computation.2 | async-start | bytes 15974400 | tf_op jit(solution)/shard_map/all_gather | solution.py:122
  11.1 355.5 %reduce-scatter.2.cloned.1.call-start = ((), (), s32[]{:S(2)}) async-start(), calls=%async_computation.3 | async-start | bytes 1310720 | tf_op jit(solution)/shard_map/reduce_scatter | solution.py:129
  65.0 49.9 %copy-start.2 = (bf16[4,64,480]{2,1,0:T(8,128)(2,1)}, bf16[4,64,480]{2,1,0:T(8,128)(2,1)S(1)}, u32[]{:S(2)}) copy-start(bf16[4,64,480]{2,1,0:T(8,128)(2,1)S(1)} %fusion.1) | copy-start | bytes 737284
  65.0 13.7 %collective-permute-start = (bf16[4,64,480]{2,1,0:T(8,128)(2,1)S(1)}, bf16[4,64,480]{2,1,0:T(8,128)(2,1)S(1)}, u32[]{:S(2)}, u32[]{:S(2)}) collective-permute-start(bf16[4,64,480]{2,1,0:T(8,128)(2,1)S(1)} %fusion.1), channel_id=1, source_target_pairs={{0,4},{4,8},{8,12},{12,16},{16,20},{20,24},{24,28},{28,32},{32,36}... | collective-permute-start | bytes 737288 | tf_op jit(solution)/shard_map/ppermute | solution.py:20
  70.1 12.7 %collective-permute-start.1 = (bf16[4,64,480]{2,1,0:T(8,128)(2,1)S(1)}, bf16[4,64,480]{2,1,0:T(8,128)(2,1)}, u32[]{:S(2)}, u32[]{:S(2)}) collective-permute-start(bf16[4,64,480]{2,1,0:T(8,128)(2,1)S(1)} %fusion.1), channel_id=1, source_target_pairs={{4,0},{8,4},{12,8},{16,12},{20,16},{24,20},{28,24},{32,28},{36,32}... | collective-permute-start | bytes 737288 | tf_op jit(solution)/shard_map/ppermute | solution.py:23
  337.5 3.2 copy-start.3
  340.7 4.1 copy-start.5
  344.5 24.4 %copy-start.4 = (s32[1,64,100]{2,1,0:T(8,128)S(1)}, s32[1,64,100]{2,1,0:T(8,128)}, u32[]{:S(2)}) copy-start(s32[1,64,100]{2,1,0:T(8,128)} %param.23) | copy-start | bytes 76804
  344.5 65.8 %all-gather.6.cloned.1.call-start = ((), (), s32[]{:S(2)}) async-start(), calls=%async_computation.4 | async-start | bytes 2228224 | tf_op jit(solution)/shard_map/all_gather | solution.py:136
  366.5 43.8 %copy-start.1 = (f32[1,64,1024]{2,1,0:T(8,128)S(1)}, f32[1,64,1024]{2,1,0:T(8,128)}, u32[]{:S(2)}) copy-start(f32[1,64,1024]{2,1,0:T(8,128)} %reduce-scatter.2.cloned.1.call-done) | copy-start | bytes 786436
Sparse Core Ops, SparseCore 0:
  10.6 50.5 all-reduce.1
  344.6 21.8 reduce-scatter.1
  369.0 41.2 all-gather.5
Sparse Core Ops, SparseCore 1:
  13.7 101.2 all-gather.3
where the time goes:
time: 514 us; the launch traced here: 506 us
  local copies, waits for them, and re-layouts  267 us (52%)
  waiting for transfers between devices  149 us (29%)
  matrix products  46.2 us (9%)
  other arithmetic  22.3 us (4%)
  between operations  14.8 us (3%)
  starting transfers between devices  7.3 us (1%)
    dynamic_slice x16, local copies, waits for them, and re-layouts, add_block(): taps = lax.dynamic_slice_in_dim(tap_block, base, joined_taps, 0)  59.7 us
    concatenate x8, local copies, waits for them, and re-layouts, add_block(): joined = jnp.concatenate(slabs, axis=-1)  57.2 us
    gather x4, local copies, waits for them, and re-layouts, utterance_loss(): neg_dot = jnp.take_along_axis(scores, neg_ids, axis=1)  48.7 us
    psum x1, waiting for transfers between devices, on_device(): summed = lax.psum(conv_term, 'tensor')  48.5 us
    all_gather x1, waiting for transfers between devices, on_device(): all_targets = lax.all_gather(own_targets, 'seq', axis=1, tiled=True)  41.1 us
    reshape x8, local copies, waits for them, and re-layouts, add_block(): jnp.transpose(taps, (1, 0, 2, 3))  36.6 us
    gather x3, local copies, waits for them, and re-layouts, utterance_loss(): neg_norm = tgt_norm[neg_ids]  35.2 us
    while x8, matrix products  30.8 us
  transfers between devices with their start and end apart: 6, of which 6 were waited for; matrix products, arithmetic and copies ran while one was open for 2% of the time, Pallas kernels for 0%

commit v1 on v0

v1 whole, which is shorter than its diff:
```python
import functools

import jax
import jax.numpy as jnp
from jax import lax
from jax.experimental import pallas as pl
from jax.experimental.pallas import tpu as pltpu
from jax.sharding import PartitionSpec as P

KERNEL = 128
MASK_LEN = 10
SHIFTS = 16
LANES = 128


ln_eps = 1e-05
norm_eps = 1e-06
logit_temp = 0.1


def exact_gelu(value):
    return 0.5 * value * (1.0 + lax.erf(value * (0.5**0.5)))


def extended(block, sides, width):
    for axis, dim in sides:
        count = lax.axis_size(axis)
        forward = [(i, i + 1) for i in range(count - 1)]
        backward = [(target, source) for source, target in forward]
        low = lax.ppermute(
            lax.slice_in_dim(block, block.shape[dim] - width, None, axis=dim), axis, forward
        )
        high = lax.ppermute(lax.slice_in_dim(block, 0, width, axis=dim), axis, backward)
        block = jnp.concatenate([low, block, high], axis=dim)
    return block


def make_targets(code_block, codebook, quant_weight):
    entries = codebook.shape[1]
    choices_row = jnp.arange(entries, dtype=jnp.int32)
    pieces = []
    for qgroup in range(codebook.shape[0]):
        onehot = (code_block[..., qgroup, None] == choices_row).astype(jnp.bfloat16)
        pieces.append(
            jnp.dot(onehot, codebook[qgroup], preferred_element_type=jnp.float32).astype(
                jnp.bfloat16
            )
        )
    codevec = jnp.concatenate(pieces, axis=-1)
    return jnp.dot(codevec, quant_weight, preferred_element_type=jnp.float32).astype(jnp.bfloat16)


def conv_body(x_ref, w_ref, fw_ref, o_ref, xf, xc, wc, acc):
    group, step = pl.program_id(0), pl.program_id(1)
    utts, rows, _ = x_ref.shape[1:]
    inner, outer = w_ref.shape[2:]
    frames = rows - KERNEL
    span = frames + SHIFTS
    kept = rows - SHIFTS

    @pl.when((group == 0) & (step == 0))
    def clear():
        wc[...] = jnp.zeros_like(wc)
        o_ref[...] = jnp.zeros_like(o_ref)

    @pl.when(step == 0)
    def shift_copies():
        acc[...] = jnp.zeros_like(acc)

        @pl.loop(0, utts)
        def one(u):
            xf[...] = x_ref[0, u].astype(jnp.float32)
            for j in range(SHIFTS):
                xc[u, :, j * LANES : (j + 1) * LANES] = xf[j : j + kept, :].astype(jnp.bfloat16)

    for half in range(2):
        for j in range(SHIFTS):
            wc[
                j * LANES : j * LANES + inner, half * LANES : half * LANES + outer
            ] = w_ref[half * SHIFTS + j, 0]
    first = pl.multiple_of(step * (2 * SHIFTS), 2 * SHIFTS)
    window = xc[:, pl.ds(first, span), :].reshape(utts * span, SHIFTS * LANES)
    acc[...] += jnp.dot(window, wc[...], preferred_element_type=jnp.float32).reshape(
        utts, span, 2 * LANES
    )

    @pl.when(step == pl.num_programs(1) - 1)
    def finish():
        conv_out = acc[:, :frames, :LANES] + acc[:, SHIFTS:, LANES:]
        own = x_ref[0, :, KERNEL // 2 : KERNEL // 2 + frames, :].astype(jnp.float32)
        mixed = (own + exact_gelu(conv_out)).astype(jnp.bfloat16)
        mixed = mixed.reshape(utts * frames, LANES)[:, :inner]
        o_ref[...] += jnp.dot(mixed, fw_ref[0], preferred_element_type=jnp.float32)


def conv_context(windows, taps, final_weight):
    groups, utts, rows, _ = windows.shape
    count, _, inner, outer = taps.shape
    frames = rows - KERNEL
    span = frames + SHIFTS
    steps = count // (2 * SHIFTS)
    code_dim = final_weight.shape[-1]
    return pl.pallas_call(
        conv_body,
        grid=(groups, steps),
        out_shape=jax.ShapeDtypeStruct((utts * frames, code_dim), jnp.float32),
        in_specs=[
            pl.BlockSpec((1, utts, rows, LANES), lambda g, p: (g, 0, 0, 0)),
            pl.BlockSpec((2 * SHIFTS, 1, inner, outer), lambda g, p: (p, g, 0, 0)),
            pl.BlockSpec((1, inner, code_dim), lambda g, p: (g, 0, 0)),
        ],
        out_specs=pl.BlockSpec((utts * frames, code_dim), lambda g, p: (0, 0)),
        scratch_shapes=[
            pltpu.VMEM((rows, LANES), jnp.float32),
            pltpu.VMEM((utts, rows - SHIFTS, SHIFTS * LANES), jnp.bfloat16),
            pltpu.VMEM((SHIFTS * LANES, 2 * LANES), jnp.bfloat16),
            pltpu.VMEM((utts, span, 2 * LANES), jnp.float32),
        ],
        compiler_params=pltpu.CompilerParams(vmem_limit_bytes=56 * 2**20),
        cost_estimate=pl.CostEstimate(
            flops=2 * utts * frames * count * groups * inner * outer,
            bytes_accessed=taps.size * 2,
            transcendentals=0,
        ),
    )(windows, taps, final_weight)


def loss_body(c_ref, t_ref, own_ref, tn_ref, count_ref, mask_ref, o_ref):
    context = c_ref[...]
    scores = lax.dot_general(
        context, t_ref[...], (((1,), (1,)), ((), ())), preferred_element_type=jnp.float32
    )
    wide = context.astype(jnp.float32)
    own = own_ref[...].astype(jnp.float32)
    ctx_norm = jnp.sum(wide * wide, axis=-1, keepdims=True) + norm_eps
    own_norm = jnp.sum(own * own, axis=-1, keepdims=True) + norm_eps
    pos_dot = jnp.sum(wide * own, axis=-1, keepdims=True)
    positive = pos_dot * lax.rsqrt(ctx_norm * own_norm) / logit_temp
    logits = scores * lax.rsqrt(ctx_norm * (tn_ref[...] + norm_eps)) / logit_temp
    total = jnp.sum(count_ref[...] * jnp.exp(logits), axis=-1, keepdims=True)
    loss = jnp.log(jnp.exp(positive) + total) - positive
    o_ref[...] = jnp.where(mask_ref[...] > 0, loss, 0.0)


def on_device(
    feature_in,
    conv_weight,
    proj_weight,
    mask_embed,
    pos_weight,
    final_weight,
    codebook,
    quant_weight,
    mask_starts,
    code_choice,
    negative_ids,
):
    utt_count, sample_rows, channels = feature_in.shape
    frames = sample_rows // 2
    utt_rows = utt_count // lax.axis_size("tensor")
    seq_count = lax.axis_size("seq")

    all_codes = lax.all_gather(code_choice.reshape(-1), "seq", axis=0, tiled=True)
    all_codes = all_codes.reshape(seq_count * frames, code_choice.shape[-1])
    taps = lax.all_gather(pos_weight, ("dp", "seq"), axis=0, tiled=True)

    frame_pairs = feature_in.reshape(utt_count, frames, 2 * channels)
    conv_term = jnp.dot(
        frame_pairs,
        conv_weight.reshape(2 * channels, conv_weight.shape[2]),
        preferred_element_type=jnp.float32,
    )
    summed = lax.psum(conv_term, "tensor")
    row_mean = jnp.mean(summed, axis=-1, keepdims=True)
    row_square = jnp.mean(summed * summed, axis=-1, keepdims=True)
    normed = (summed - row_mean) * lax.rsqrt(row_square - row_mean * row_mean + ln_eps)
    features = jax.nn.gelu(normed, approximate=False).astype(jnp.bfloat16)
    projected = jnp.dot(features, proj_weight, preferred_element_type=jnp.float32).astype(
        jnp.bfloat16
    )
    positions = (lax.axis_index("seq") * frames + jnp.arange(frames, dtype=jnp.int32))[
        None, :, None
    ]
    starts = mask_starts[:, None, :]
    masked = jnp.any((positions >= starts) & (positions < starts + MASK_LEN), axis=-1)
    hidden = jnp.where(masked[..., None], mask_embed[None, None, :], projected)
    padded = extended(hidden, (("seq", 1),), KERNEL // 2)

    all_targets = make_targets(all_codes, codebook, quant_weight)
    wide_targets = all_targets.astype(jnp.float32)
    tgt_norm = jnp.sum(wide_targets * wide_targets, axis=-1)[None, :]
    own_targets = lax.dynamic_slice_in_dim(
        all_targets, lax.axis_index("seq") * frames, frames, 0
    )
    ids = negative_ids.reshape(frames, negative_ids.shape[-1])
    frame_row = jnp.arange(seq_count * frames, dtype=jnp.int32)
    counts = jnp.sum((ids[:, :, None] == frame_row).astype(jnp.float32), axis=1)
    padded, all_targets, own_targets, tgt_norm, counts = lax.optimization_barrier(
        (padded, all_targets, own_targets, tgt_norm, counts)
    )

    group_count, inner = pos_weight.shape[1], pos_weight.shape[2]
    windows = padded.reshape(utt_count, padded.shape[1], group_count, inner)
    windows = jnp.pad(windows.transpose(2, 0, 1, 3), ((0, 0), (0, 0), (0, 0), (0, LANES - inner)))
    partial = conv_context(
        windows, taps, final_weight.reshape(group_count, inner, final_weight.shape[1])
    )
    context = lax.psum_scatter(partial, "tensor", scatter_dimension=0, tiled=True).astype(
        jnp.bfloat16
    )
    is_masked = lax.dynamic_slice_in_dim(masked, lax.axis_index("tensor") * utt_rows, utt_rows, 0)
    loss = pl.pallas_call(
        loss_body,
        out_shape=jax.ShapeDtypeStruct((utt_rows * frames, 1), jnp.float32),
        compiler_params=pltpu.CompilerParams(vmem_limit_bytes=24 * 2**20),
    )(
        context,
        all_targets,
        own_targets,
        tgt_norm,
        counts,
        is_masked.reshape(utt_rows * frames, 1).astype(jnp.float32),
    )
    return loss.reshape(utt_rows, frames)


def solution(mesh):
    return jax.shard_map(
        on_device,
        mesh=mesh,
        in_specs=(
            P("dp", "seq", "tensor"),
            P(None, "tensor", None),
            P(None, "tensor"),
            P("tensor"),
            P(("dp", "seq"), "tensor", None, None),
            P("tensor", None),
            P(),
            P(),
            P("dp", None),
            P(("dp", "tensor"), "seq", None),
            P(("dp", "tensor"), "seq", None),
        ),
        out_specs=P(("dp", "tensor"), "seq"),
        check_vma=False,
    )
```

time: 514 us -> 170 us (0.33); the launches traced: 506 us -> 168 us
  local copies, waits for them, and re-layouts: 267 us -> 10.8 us
  waiting for transfers between devices: 149 us -> 74.7 us
  matrix products: 46.2 us -> 9.99 us
  blocking collectives: 0 us -> 21.2 us
  Pallas kernels: 0 us -> 20.6 us
  other arithmetic: 22.3 us -> 8.87 us
    gather x7 -> x0, local copies, waits for them, and re-layouts: 83.8 us -> none  [the longest x4 48.7 us: utterance_loss(): neg_dot = jnp.take_along_axis(scores, neg_ids, axis=1)]
    dynamic_slice x24 -> x1, local copies, waits for them, and re-layouts: 83.4 us -> 0.92 us  [on_device(): lax.dynamic_slice_in_dim(all_targets, lax.axis_index('seq') * frames, fra...]
    concatenate x8 -> x0, local copies, waits for them, and re-layouts: 57.2 us -> none  [add_block(): joined = jnp.concatenate(slabs, axis=-1)]
    all_gather x2 -> x1, waiting for transfers between devices: 69.4 us -> 27.1 us  [on_device(): taps = lax.all_gather(pos_weight, ('dp', 'seq'), axis=0, tiled=True)]
    reshape x8 -> x1, local copies, waits for them, and re-layouts: 36.6 us -> 0.46 us  [on_device(): all_codes = all_codes.reshape(seq_count * frames, code_choice.shape[-1])]
    while x8 -> x0, matrix products: 30.8 us -> none
    psum x1, waiting for transfers between devices: 48.5 us -> 19.9 us  [on_device(): summed = lax.psum(conv_term, 'tensor')]
    all_gather x0 -> x1, blocking collectives: none -> 21.2 us  [on_device(): lax.all_gather(code_choice.reshape(-1), 'seq', axis=0, tiled=True)]
  transfers between devices with their start and end apart: 6 -> 5, of which waited for: 6 -> 5; matrix products, arithmetic and copies ran while one was open for 2% -> 13% of each run, Pallas kernels for 0% -> 0%
where the time goes in v1:
time: 170 us; the launch traced here: 168 us
  waiting for transfers between devices  74.7 us (44%)
  blocking collectives  21.2 us (12%)
  Pallas kernels  20.6 us (12%)
  between operations  15.1 us (9%)
  local copies, waits for them, and re-layouts  10.8 us (6%)
  matrix products  9.99 us (6%)
  other arithmetic  8.87 us (5%)
  starting transfers between devices  7.11 us (4%)
    all_gather x1, waiting for transfers between devices, on_device(): taps = lax.all_gather(pos_weight, ('dp', 'seq'), axis=0, tiled=True)  27.1 us
    reduce_scatter x1, waiting for transfers between devices, on_device(): lax.psum_scatter(partial, 'tensor', scatter_dimension=0, tiled=True)  21.9 us
    all_gather x1, blocking collectives, on_device(): lax.all_gather(code_choice.reshape(-1), 'seq', axis=0, tiled=True)  21.2 us
    psum x1, waiting for transfers between devices, on_device(): summed = lax.psum(conv_term, 'tensor')  19.9 us
    pallas_call x1, Pallas kernels, conv_context(): pl.pallas_call(conv_body, grid=(groups, steps), out_shape=jax.ShapeDtypeS...  19.8 us
    ppermute x1, starting transfers between devices, extended(): lax.ppermute(lax.slice_in_dim(block, block.shape[dim] - width, None, axis...  5.07 us
    reduce_sum x1, other arithmetic, on_device(): counts = jnp.sum((ids[:, :, None] == frame_row).astype(jnp.float32), axis=1)  4.04 us
    dot_general x1, matrix products, make_targets(): jnp.dot(codevec, quant_weight, preferred_element_type=jnp.float32)  3.76 us
  transfers between devices with their start and end apart: 5, of which 5 were waited for; matrix products, arithmetic and copies ran while one was open for 13% of the time, Pallas kernels for 0%

profile of v1, /device:TPU:1, one launch (start us, length us, event | category | flops | bytes accessed | tf_op | source)
XLA Modules:
  0.0 168.3 jit_solution(15539858801895349576)
XLA Ops:
  7.4 1.1 reshape.64
  8.5 2.0 %fusion.95 = f32[4,64,512]{2,1,0:T(8,128)} fusion(bf16[4,64,256]{2,1,0:T(8,128)(2,1)S(1)} %reshape.64, bf16[256,512,1]{1,0,2:T(8,128)(2,1)} %bitcast.27), kind=kOutput, calls=%fused_computation.120 | convolution fusion | flops 67108864 | bytes 917504 | tf_op jit(solution)/shard_map/dot_general | solution.py:168
  10.6 0.5 all-gather.3.cloned.1.call-update
  11.2 0.8 copy.20
  12.1 21.2 %all-gather = s32[16,1,128]{2,1,0:T(1,128)S(1)} all-gather(s32[1,1,128]{2,1,0:T(1,128)S(1)} %reshape.72), channel_id=1, replica_groups=mesh['dp'=4,'seq'=16,'tensor'=4] {'seq'}, dimensions={0}, use_global_device_ids=true | all-gather | bytes 8704 | tf_op jit(solution)/shard_map/all_gather | solution.py:163
  33.3 0.5 broadcast.53
  33.8 0.7 reduce.8
  35.3 0.5 slice_reduce_fusion.1
  35.8 0.9 fusion.10
  36.7 0.9 fusion.9
  37.6 3.8 %multiply_reduce_fusion = (f32[1024]{0:T(1024)S(1)}, bf16[1024,1024]{1,0:T(8,128)(2,1)}) fusion(bf16[1024,1024]{1,0:T(8,128)(2,1)S(1)} %copy-done, bf16[1024,512]{0,1:T(8,128)(2,1)S(1)} %fusion.9, bf16[1024,512]{0,1:T(8,128)(2,1)S(1)} %fusion.10), kind=kOutput, calls=%fused_computation.2 | convolution fusion | flops 2155871232 | bytes 6295552 | tf_op jit(solution)/shard_map/dot_general | solution.py:50
  41.4 19.9 %all-reduce.3.cloned.1.call-done = f32[4,64,512]{2,1,0:T(8,128)} async-done(((f32[4,64,512]{2,1,0:T(8,128)}), f32[4,64,512]{2,1,0:T(8,128)}) %all-reduce.3.cloned.1.call-update) | async-done | bytes 524304 | tf_op jit(solution)/shard_map/psum | solution.py:173
  61.3 1.2 fusion.94
  62.5 2.4 %fusion.11 = bf16[4,64,480]{2,1,0:T(8,128)(2,1)S(1)} fusion(bf16[512,480]{0,1:T(8,128)(2,1)S(1)} %copy-done.6, f32[4,64,512]{2,1,0:T(8,128)} %all-reduce.3.cloned.1.call-done, f32[4,64]{1,0:T(4,128)S(1)} %get-tuple-element.20, f32[4,64]{1,0:T(4,128)S(1)} %get-tuple-element.19, pred[4,64]{1,0:T(4,128)(4,1)S(1)} %and_reduce_fusion, ...), kind=kOutput, calls=%fused_computation.15 | convolution fusion | flops 134856704 | bytes 1264832 | tf_op jit(solution)/shard_map/dot_general | solution.py:178
  65.0 5.1 %collective-permute-start = (bf16[4,64,480]{2,1,0:T(8,128)(2,1)S(1)}, bf16[4,64,480]{2,1,0:T(8,128)(2,1)S(1)}, u32[]{:S(2)}, u32[]{:S(2)}) collective-permute-start(bf16[4,64,480]{2,1,0:T(8,128)(2,1)S(1)} %fusion.11), channel_id=1, source_target_pairs={{0,4},{4,8},{8,12},{12,16},{16,20},{20,24},{24,28},{28,32},{32,36}... | collective-permute-start | bytes 737288 | tf_op jit(solution)/shard_map/ppermute | solution.py:30
  70.0 1.9 %collective-permute-start.1 = (bf16[4,64,480]{2,1,0:T(8,128)(2,1)S(1)}, bf16[4,64,480]{2,1,0:T(8,128)(2,1)}, u32[]{:S(2)}, u32[]{:S(2)}) collective-permute-start(bf16[4,64,480]{2,1,0:T(8,128)(2,1)S(1)} %fusion.11), channel_id=1, source_target_pairs={{4,0},{8,4},{12,8},{16,12},{20,16},{24,20},{28,24},{32,28},{36,32}... | collective-permute-start | bytes 737288 | tf_op jit(solution)/shard_map/ppermute | solution.py:33
  72.0 4.0 %convert_reduce_fusion.count_ref = f32[64,1024]{1,0:T(8,128)S(1)} fusion(s32[64,100]{0,1:T(8,128)S(1)} %copy.21), kind=kLoop, calls=%fused_computation | loop fusion | flops 19595264 | bytes 287744 | tf_op jit(solution)/shard_map/reduce_sum | solution.py:197
  76.0 0.9 constant_dynamic-slice_fusion.own_ref
  76.9 1.8 %collective-permute-done = bf16[4,64,480]{2,1,0:T(8,128)(2,1)S(1)} collective-permute-done((bf16[4,64,480]{2,1,0:T(8,128)(2,1)S(1)}, bf16[4,64,480]{2,1,0:T(8,128)(2,1)S(1)}, u32[]{:S(2)}, u32[]{:S(2)}) %collective-permute-start) | collective-permute-done | bytes 245792 | tf_op jit(solution)/shard_map/ppermute | solution.py:30
  78.7 0.7 copy-done.2
  79.4 3.5 %collective-permute-done.1 = bf16[4,64,480]{2,1,0:T(8,128)(2,1)} collective-permute-done((bf16[4,64,480]{2,1,0:T(8,128)(2,1)S(1)}, bf16[4,64,480]{2,1,0:T(8,128)(2,1)}, u32[]{:S(2)}, u32[]{:S(2)}) %collective-permute-start.1) | collective-permute-done | bytes 245792 | tf_op jit(solution)/shard_map/ppermute | solution.py:33
  82.9 1.2 pad_maximum_fusion
  84.1 1.4 reshape.68
  85.5 1.3 copy.25
  86.8 1.1 pad.4.x_ref
  87.9 27.1 %all-gather.3.cloned.1.call-done.w_ref = bf16[128,4,120,120]{3,2,1,0:T(8,128)(2,1)} async-done(((bf16[2,4,120,120]{3,2,1,0:T(8,128)(2,1)}), bf16[128,4,120,120]{3,2,1,0:T(8,128)(2,1)}) %all-gather.3.cloned.1.call-update) | async-done | bytes 14745616 | tf_op jit(solution)/shard_map/all_gather | solution.py:165
  115.0 19.8 %shard_map.109 = f32[256,1024]{1,0:T(8,128)} custom-call(bf16[4,4,192,128]{3,2,1,0:T(8,128)(2,1)} %pad.4.x_ref, bf16[128,4,120,120]{3,2,1,0:T(8,128)(2,1)} %all-gather.3.cloned.1.call-done.w_ref, bf16[4,120,1024]{2,1,0:T(8,128)(2,1)} %bitcast.26), custom_call_target="tpu_custom_call" | custom-call | flops 3774873600 | bytes 14745600 | tf_op jit(solution)/shard_map/pallas_call | solution.py:103
  134.9 21.9 %reduce-scatter.2.cloned.1.call-done = f32[64,1024]{1,0:T(8,128)} async-done(((f32[256,1024]{1,0:T(8,128)}), f32[64,1024]{1,0:T(8,128)}) %reduce-scatter.2.cloned.1.call-update) | async-done | bytes 262160 | tf_op jit(solution)/shard_map/reduce_scatter | solution.py:208
  156.8 1.0 convert_element_type.40.c_ref
  157.8 1.6 copy-done.1
  159.4 0.9 shard_map.110
  160.2 0.6 reduce.3
  (28 shorter events, 1.2 us)
Async XLA Ops:
  7.4 30.2 %copy-start = (bf16[1024,1024]{1,0:T(8,128)(2,1)S(1)}, bf16[1024,1024]{1,0:T(8,128)(2,1)}, u32[]{:S(2)}) copy-start(bf16[1024,1024]{1,0:T(8,128)(2,1)} %param.18) | copy-start | bytes 6291460
  7.4 27.6 %copy-start.3 = (s32[1,64,100]{2,1,0:T(8,128)S(1)}, s32[1,64,100]{2,1,0:T(8,128)}, u32[]{:S(2)}) copy-start(s32[1,64,100]{2,1,0:T(8,128)} %param.21) | copy-start | bytes 76804
  7.4 27.7 %copy-start.4 = (s32[4,66]{1,0:T(4,128)S(1)}, s32[4,66]{1,0:T(4,128)}, u32[]{:S(2)}) copy-start(s32[4,66]{1,0:T(4,128)} %param.19) | copy-start | bytes 3172
  7.4 28.4 %copy-start.5 = (bf16[2,320,512]{2,1,0:T(8,128)(2,1)S(1)}, bf16[2,320,512]{2,1,0:T(8,128)(2,1)}, u32[]{:S(2)}) copy-start(bf16[2,320,512]{2,1,0:T(8,128)(2,1)} %param.17) | copy-start | bytes 1966084
  7.4 53.9 %all-reduce.3.cloned.1.call-start = ((), (), s32[]{:S(2)}) async-start(), calls=%async_computation.1 | async-start | bytes 1048576 | tf_op jit(solution)/shard_map/psum | solution.py:173
  10.6 104.4 %all-gather.3.cloned.1.call-start = ((), (), s32[]{:S(2)}) async-start(), calls=%async_computation.2 | async-start | bytes 15974400 | tf_op jit(solution)/shard_map/all_gather | solution.py:165
  11.1 145.7 %reduce-scatter.2.cloned.1.call-start = ((), (), s32[]{:S(2)}) async-start(), calls=%async_computation.3 | async-start | bytes 1310720 | tf_op jit(solution)/shard_map/reduce_scatter | solution.py:208
  37.6 24.9 %copy-start.6 = (bf16[512,480]{0,1:T(8,128)(2,1)S(1)}, bf16[512,480]{0,1:T(8,128)(2,1)}, u32[]{:S(2)}) copy-start(bf16[512,480]{0,1:T(8,128)(2,1)} %param.13) | copy-start | bytes 1474564
  37.6 24.9 %copy-start.7 = (bf16[480]{0:T(512)(128)(2,1)S(1)}, bf16[480]{0:T(512)(128)(2,1)}, u32[]{:S(2)}) copy-start(bf16[480]{0:T(512)(128)(2,1)} %param.14) | copy-start | bytes 2884
  65.0 13.8 %collective-permute-start = (bf16[4,64,480]{2,1,0:T(8,128)(2,1)S(1)}, bf16[4,64,480]{2,1,0:T(8,128)(2,1)S(1)}, u32[]{:S(2)}, u32[]{:S(2)}) collective-permute-start(bf16[4,64,480]{2,1,0:T(8,128)(2,1)S(1)} %fusion.11), channel_id=1, source_target_pairs={{0,4},{4,8},{8,12},{12,16},{16,20},{20,24},{24,28},{28,32},{32,36}... | collective-permute-start | bytes 737288 | tf_op jit(solution)/shard_map/ppermute | solution.py:30
  70.0 12.9 %collective-permute-start.1 = (bf16[4,64,480]{2,1,0:T(8,128)(2,1)S(1)}, bf16[4,64,480]{2,1,0:T(8,128)(2,1)}, u32[]{:S(2)}, u32[]{:S(2)}) collective-permute-start(bf16[4,64,480]{2,1,0:T(8,128)(2,1)S(1)} %fusion.11), channel_id=1, source_target_pairs={{4,0},{8,4},{12,8},{16,12},{20,16},{24,20},{28,24},{32,28},{36,32}... | collective-permute-start | bytes 737288 | tf_op jit(solution)/shard_map/ppermute | solution.py:33
  78.7 0.7 copy-start.2
  157.8 1.6 copy-start.1
Sparse Core Ops, SparseCore 0:
  10.7 50.5 all-reduce.2
  134.9 21.8 reduce-scatter.1
Sparse Core Ops, SparseCore 1:
  13.8 101.2 all-gather.2

commit v2 on v1

v2 whole, which is shorter than its diff:
```python
import functools

import jax
import jax.numpy as jnp
from jax import lax
from jax.experimental import pallas as pl
from jax.experimental.pallas import tpu as pltpu
from jax.sharding import PartitionSpec as P

KERNEL = 128
MASK_LEN = 10
SHIFTS = 16
LANES = 128


ln_eps = 1e-05
norm_eps = 1e-06
logit_temp = 0.1


def exact_gelu(value):
    return 0.5 * value * (1.0 + lax.erf(value * (0.5**0.5)))


def make_targets(code_block, codebook, quant_weight):
    entries = codebook.shape[1]
    choices_row = jnp.arange(entries, dtype=jnp.int32)
    pieces = []
    for qgroup in range(codebook.shape[0]):
        onehot = (code_block[..., qgroup, None] == choices_row).astype(jnp.bfloat16)
        pieces.append(
            jnp.dot(onehot, codebook[qgroup], preferred_element_type=jnp.float32).astype(
                jnp.bfloat16
            )
        )
    codevec = jnp.concatenate(pieces, axis=-1)
    return jnp.dot(codevec, quant_weight, preferred_element_type=jnp.float32).astype(jnp.bfloat16)


def remote(src, dst, send, recv, **coords):
    return pltpu.make_async_remote_copy(
        src_ref=src,
        dst_ref=dst,
        send_sem=send,
        recv_sem=recv,
        device_id=coords,
        device_id_type=pl.DeviceIdType.MESH,
    )


def greet(barrier, **coords):
    pl.semaphore_signal(
        barrier, inc=1, device_id=coords, device_id_type=pl.DeviceIdType.MESH
    )


def front_body(
    sizes,
    pairs_ref,
    cw_ref,
    pw_ref,
    embed_ref,
    mask_ref,
    taps_in,
    codes_in,
    win_ref,
    taps_ref,
    codes_ref,
    term_wide,
    term_half,
    arrived,
    feat,
    hidden,
    local_sem,
    code_send,
    code_recv,
    tap_send,
    tap_recv,
    ring_send,
    ring_recv,
    pair_send,
    pair_recv,
    sum_send,
    sum_recv,
    feat_send,
    feat_recv,
    win_send,
    win_recv,
):
    dps, seqs, tensors = sizes
    chips = seqs // 2
    dp, seq, tensor = (lax.axis_index(name) for name in ("dp", "seq", "tensor"))
    utts, frames, channels = term_wide.shape

    def other_dp(k):
        return lax.rem(dp + k, dps)

    def other_seq(k):
        return lax.rem(seq + (k + seqs) % seqs, seqs)

    def other_tensor(k):
        return lax.rem(tensor + k, tensors)

    barrier = pltpu.get_barrier_semaphore()
    for k in range(1, seqs):
        greet(barrier, seq=other_seq(k))
    for k in range(1, dps):
        for side in (-1, 0, 1):
            greet(barrier, dp=other_dp(k), seq=other_seq(side))
    for k in range(1, tensors):
        greet(barrier, tensor=other_tensor(k))
    pl.semaphore_wait(barrier, (seqs - 1) + 3 * (dps - 1) + (tensors - 1))

    pending = []

    def begin(copy):
        copy.start()
        pending.append(copy)
        return copy

    local = pltpu.make_async_copy(taps_in.at[:, dp], taps_ref.at[dp, seq], local_sem.at[0])
    local.start()
    tap_copies = [
        begin(
            remote(
                taps_in.at[:, other_dp(k)],
                taps_ref.at[dp, seq],
                tap_send.at[k - 1],
                tap_recv.at[k - 1],
                dp=other_dp(k),
            )
        )
        for k in range(1, dps)
    ]
    code_copies = [
        begin(
            remote(
                codes_in,
                codes_ref.at[seq],
                code_send.at[k - 1],
                code_recv.at[k - 1],
                seq=other_seq(k),
            )
        )
        for k in range(1, seqs)
    ]
    codes_ref[seq] = codes_in[...]

    term = jnp.dot(pairs_ref[...], cw_ref[...], preferred_element_type=jnp.float32)
    term = term.reshape(utts, frames, channels)
    term_wide[...] = term
    term_half[...] = term.astype(jnp.bfloat16)
    sum_copies = [
        begin(
            remote(
                term_half.at[other_tensor(k)],
                arrived.at[k - 1],
                sum_send.at[k - 1],
                sum_recv.at[k - 1],
                tensor=other_tensor(k),
            )
        )
        for k in range(1, tensors)
    ]

    local.wait()
    for copy in tap_copies:
        copy.wait_recv()

    core = lax.rem(seq, 2)
    sibling = seq + 1 - 2 * core

    def pass_block(slot, hop):
        block = taps_ref.at[:, lax.rem(seq + 2 * hop + seqs, seqs)]
        return begin(
            remote(block, block, pair_send.at[slot], pair_recv.at[slot], seq=sibling)
        )

    def ring(slot, hop, direction):
        block = taps_ref.at[:, lax.rem(seq + 2 * hop + seqs, seqs)]
        return begin(
            remote(
                block,
                block,
                ring_send.at[slot],
                ring_recv.at[slot],
                seq=other_seq(2 * direction),
            )
        )

    ups, downs = chips // 2, (chips - 1) // 2
    pair_copies = [pass_block(0, 0)]
    up = [ring(0, 0, 1)]
    down = [ring(ups, 0, -1)]

    def advance(step):
        if step - 1 < ups:
            up[step - 1].wait_recv()
            pair_copies.append(pass_block(step, -step))
            if step < ups:
                up.append(ring(step, -step, 1))
        if step - 1 < downs:
            down[step - 1].wait_recv()
            pair_copies.append(pass_block(ups + step, step))
            if step < downs:
                down.append(ring(ups + step, step, -1))

    summed = term_wide[tensor]
    for k, copy in enumerate(sum_copies):
        copy.wait_recv()
        summed = summed + arrived[k].astype(jnp.float32)
    row_mean = jnp.mean(summed, axis=-1, keepdims=True)
    row_square = jnp.mean(summed * summed, axis=-1, keepdims=True)
    normed = (summed - row_mean) * lax.rsqrt(row_square - row_mean * row_mean + ln_eps)
    feat[tensor] = exact_gelu(normed).astype(jnp.bfloat16)
    feat_copies = [
        begin(
            remote(
                feat.at[tensor],
                feat.at[tensor],
                feat_send.at[k - 1],
                feat_recv.at[k - 1],
                tensor=other_tensor(k),
            )
        )
        for k in range(1, tensors)
    ]
    advance(1)
    for copy in feat_copies:
        copy.wait_recv()
    features = feat[...].reshape(utts * frames, channels)
    is_masked = mask_ref[...] > 0
    for group in range(dps):
        projected = jnp.dot(features, pw_ref[group], preferred_element_type=jnp.float32)
        chosen = jnp.where(is_masked, embed_ref[group].astype(jnp.float32), projected)
        hidden[group] = chosen.astype(jnp.bfloat16).reshape(utts, frames, LANES)
    mine = pl.ds(dp * utts, utts)
    win_copies = []
    for k in range(dps):
        for side in (-1, 0, 1):
            slot = 3 * k + side + 1
            if k == 0 and side == 0:
                continue
            win_copies.append(
                begin(
                    remote(
                        hidden.at[other_dp(k)],
                        win_ref.at[mine, 1 - side],
                        win_send.at[slot],
                        win_recv.at[slot],
                        dp=other_dp(k),
                        seq=other_seq(side),
                    )
                )
            )
    win_ref[mine, 1] = hidden[dp]
    advance(2)
    for copy in win_copies:
        copy.wait_recv()

    @pl.when(seq == 0)
    def low_edge():
        win_ref[:, 0] = jnp.zeros_like(win_ref[:, 0])

    @pl.when(seq == seqs - 1)
    def high_edge():
        win_ref[:, 2] = jnp.zeros_like(win_ref[:, 2])

    for step in range(3, ups + 1):
        advance(step)
    for copy in pair_copies + code_copies:
        copy.wait_recv()
    for copy in pending:
        copy.wait_send()


def front(sizes, utts, pairs, cw, pw, embed, mask, taps, codes):
    dps, seqs, tensors = sizes
    frames = mask.shape[0] // utts
    channels = cw.shape[1]
    per, _, inner, outer = taps.shape
    vmem = pl.BlockSpec(memory_space=pltpu.VMEM)
    dma = pltpu.SemaphoreType.DMA
    hops = seqs // 2
    return pl.pallas_call(
        functools.partial(front_body, sizes),
        out_shape=(
            jax.ShapeDtypeStruct((utts * dps, 3, frames, LANES), jnp.bfloat16),
            jax.ShapeDtypeStruct((dps, seqs, per, inner, outer), jnp.bfloat16),
            jax.ShapeDtypeStruct((seqs,) + codes.shape, codes.dtype),
        ),
        in_specs=[vmem] * 7,
        out_specs=(vmem, pl.BlockSpec(memory_space=pl.ANY), vmem),
        scratch_shapes=[
            pltpu.VMEM((utts, frames, channels), jnp.float32),
            pltpu.VMEM((utts, frames, channels), jnp.bfloat16),
            pltpu.VMEM((tensors - 1, frames, channels), jnp.bfloat16),
            pltpu.VMEM((utts, frames, channels), jnp.bfloat16),
            pltpu.VMEM((dps, utts, frames, LANES), jnp.bfloat16),
            dma((1,)),
            dma((seqs - 1,)),
            dma((seqs - 1,)),
            dma((dps - 1,)),
            dma((dps - 1,)),
            dma((hops - 1,)),
            dma((hops - 1,)),
            dma((hops,)),
            dma((hops,)),
            dma((tensors - 1,)),
            dma((tensors - 1,)),
            dma((tensors - 1,)),
            dma((tensors - 1,)),
            dma((3 * dps,)),
            dma((3 * dps,)),
        ],
        compiler_params=pltpu.CompilerParams(
            collective_id=0, has_side_effects=True, vmem_limit_bytes=40 * 2**20
        ),
    )(pairs, cw, pw, embed, mask, taps, codes)


def conv_body(x_ref, w_ref, o_ref, xf, xc, wc, acc):
    step = pl.program_id(0)
    utts, rows, _ = x_ref.shape
    inner, outer = w_ref.shape[1:]
    frames = rows - KERNEL
    span = frames + SHIFTS
    kept = rows - SHIFTS
    joint = 4

    @pl.when(step == 0)
    def shift_copies():
        wc[...] = jnp.zeros_like(wc)
        acc[...] = jnp.zeros_like(acc)

        @pl.loop(0, utts)
        def one(u):
            xf[...] = x_ref[u].astype(jnp.float32)
            for j in range(SHIFTS):
                xc[u, :, j * LANES : (j + 1) * LANES] = xf[j : j + kept, :].astype(jnp.bfloat16)

    for half in range(2):
        for j in range(SHIFTS):
            wc[
                j * LANES : j * LANES + inner, half * LANES : half * LANES + outer
            ] = w_ref[half * SHIFTS + j]
    first = pl.multiple_of(step * (2 * SHIFTS), 2 * SHIFTS)

    @pl.loop(0, utts // joint)
    def multiply(chunk):
        here = pl.ds(chunk * joint, joint)
        window = xc[here, pl.ds(first, span), :].reshape(joint * span, SHIFTS * LANES)
        acc[here] += jnp.dot(window, wc[...], preferred_element_type=jnp.float32).reshape(
            joint, span, 2 * LANES
        )

    @pl.when(step == pl.num_programs(0) - 1)
    def finish():
        @pl.loop(0, utts)
        def one(u):
            conv_out = acc[u, :frames, :LANES] + acc[u, SHIFTS:, LANES:]
            own = x_ref[u, KERNEL // 2 : KERNEL // 2 + frames, :].astype(jnp.float32)
            o_ref[u] = (own + exact_gelu(conv_out)).astype(jnp.bfloat16)


def grouped_conv(windows, taps):
    utts, rows, _ = windows.shape
    count, inner, outer = taps.shape
    frames = rows - KERNEL
    span = frames + SHIFTS
    steps = count // (2 * SHIFTS)
    return pl.pallas_call(
        conv_body,
        grid=(steps,),
        out_shape=jax.ShapeDtypeStruct((utts, frames, LANES), jnp.bfloat16),
        in_specs=[
            pl.BlockSpec((utts, rows, LANES), lambda p: (0, 0, 0)),
            pl.BlockSpec((2 * SHIFTS, inner, outer), lambda p: (p, 0, 0)),
        ],
        out_specs=pl.BlockSpec((utts, frames, LANES), lambda p: (0, 0, 0)),
        scratch_shapes=[
            pltpu.VMEM((rows, LANES), jnp.float32),
            pltpu.VMEM((utts, rows - SHIFTS, SHIFTS * LANES), jnp.bfloat16),
            pltpu.VMEM((SHIFTS * LANES, 2 * LANES), jnp.bfloat16),
            pltpu.VMEM((utts, span, 2 * LANES), jnp.float32),
        ],
        compiler_params=pltpu.CompilerParams(vmem_limit_bytes=48 * 2**20),
    )(windows, taps)


def back_body(
    sizes,
    mixed_ref,
    fw_ref,
    t_ref,
    own_ref,
    tn_ref,
    count_ref,
    mask_ref,
    o_ref,
    gathered,
    part_wide,
    part_half,
    arrived,
    mix_send,
    mix_recv,
    sum_send,
    sum_recv,
):
    dps, _, tensors = sizes
    dp, tensor = lax.axis_index("dp"), lax.axis_index("tensor")
    utts, frames, code_dim = part_wide.shape
    inner = fw_ref.shape[1]

    barrier = pltpu.get_barrier_semaphore()
    for k in range(1, dps):
        greet(barrier, dp=lax.rem(dp + k, dps))
    for k in range(1, tensors):
        greet(barrier, tensor=lax.rem(tensor + k, tensors))
    pl.semaphore_wait(barrier, dps - 1 + tensors - 1)

    mix_copies = []
    for k in range(1, dps):
        there = lax.rem(dp + k, dps)
        copy = remote(
            mixed_ref.at[pl.ds(there * utts, utts)],
            gathered.at[dp],
            mix_send.at[k - 1],
            mix_recv.at[k - 1],
            dp=there,
        )
        copy.start()
        mix_copies.append(copy)
    gathered[dp] = mixed_ref[pl.ds(dp * utts, utts)]
    for copy in mix_copies:
        copy.wait_recv()
    sum_copies = []
    for k in range(tensors):
        there = lax.rem(tensor + k + 1, tensors)
        total = jnp.zeros((frames, code_dim), jnp.float32)
        for group in range(dps):
            rows = gathered[group, there][:, :inner]
            total += jnp.dot(rows, fw_ref[group], preferred_element_type=jnp.float32)
        if k < tensors - 1:
            part_half[k] = total.astype(jnp.bfloat16)
            copy = remote(
                part_half.at[k],
                arrived.at[k],
                sum_send.at[k],
                sum_recv.at[k],
                tensor=there,
            )
            copy.start()
            sum_copies.append(copy)
    for k, copy in enumerate(sum_copies):
        copy.wait_recv()
        total += arrived[k].astype(jnp.float32)
    context = total.astype(jnp.bfloat16)
    scores = lax.dot_general(
        context, t_ref[...], (((1,), (1,)), ((), ())), preferred_element_type=jnp.float32
    )
    wide = context.astype(jnp.float32)
    own = own_ref[...].astype(jnp.float32)
    ctx_norm = jnp.sum(wide * wide, axis=-1, keepdims=True) + norm_eps
    own_norm = jnp.sum(own * own, axis=-1, keepdims=True) + norm_eps
    pos_dot = jnp.sum(wide * own, axis=-1, keepdims=True)
    positive = pos_dot * lax.rsqrt(ctx_norm * own_norm) / logit_temp
    logits = scores * lax.rsqrt(ctx_norm * (tn_ref[...] + norm_eps)) / logit_temp
    negatives = jnp.sum(count_ref[...] * jnp.exp(logits), axis=-1, keepdims=True)
    loss = jnp.log(jnp.exp(positive) + negatives) - positive
    o_ref[...] = jnp.where(mask_ref[...] > 0, loss, 0.0)
    for copy in mix_copies + sum_copies:
        copy.wait_send()


def back(sizes, mixed, fw, targets, own, norms, counts, mask):
    dps, _, tensors = sizes
    utts, frames = mixed.shape[0] // dps, mixed.shape[1]
    code_dim = fw.shape[-1]
    dma = pltpu.SemaphoreType.DMA
    return pl.pallas_call(
        functools.partial(back_body, sizes),
        out_shape=jax.ShapeDtypeStruct((frames, 1), jnp.float32),
        in_specs=[pl.BlockSpec(memory_space=pltpu.VMEM)] * 7,
        out_specs=pl.BlockSpec(memory_space=pltpu.VMEM),
        scratch_shapes=[
            pltpu.VMEM((dps, utts, frames, LANES), jnp.bfloat16),
            pltpu.VMEM((utts, frames, code_dim), jnp.float32),
            pltpu.VMEM((tensors - 1, frames, code_dim), jnp.bfloat16),
            pltpu.VMEM((tensors - 1, frames, code_dim), jnp.bfloat16),
            dma((dps - 1,)),
            dma((dps - 1,)),
            dma((tensors - 1,)),
            dma((tensors - 1,)),
        ],
        compiler_params=pltpu.CompilerParams(
            collective_id=1, has_side_effects=True, vmem_limit_bytes=32 * 2**20
        ),
    )(mixed, fw, targets, own, norms, counts, mask)


def on_device(
    feature_in,
    conv_weight,
    proj_weight,
    mask_embed,
    pos_weight,
    final_weight,
    codebook,
    quant_weight,
    mask_starts,
    code_choice,
    negative_ids,
):
    utts, sample_rows, channels = feature_in.shape
    frames = sample_rows // 2
    sizes = tuple(lax.axis_size(name) for name in ("dp", "seq", "tensor"))
    dps, seqs, tensors = sizes
    groups, inner = pos_weight.shape[1], pos_weight.shape[2]
    padding = LANES - inner

    pairs = feature_in.reshape(utts * frames, 2 * channels)
    cw = conv_weight.reshape(2 * channels, conv_weight.shape[2])
    pw = proj_weight.reshape(proj_weight.shape[0], groups, inner).transpose(1, 0, 2)
    pw = jnp.pad(pw, ((0, 0), (0, 0), (0, padding)))
    embed = jnp.pad(mask_embed.reshape(groups, 1, inner), ((0, 0), (0, 0), (0, padding)))
    positions = (lax.axis_index("seq") * frames + jnp.arange(frames, dtype=jnp.int32))[
        None, :, None
    ]
    starts = mask_starts[:, None, :]
    masked = jnp.any((positions >= starts) & (positions < starts + MASK_LEN), axis=-1)
    masked = masked.astype(jnp.float32).reshape(utts * frames, 1)

    windows, taps, codes = front(
        sizes,
        utts,
        pairs,
        cw,
        pw,
        embed,
        masked,
        pos_weight,
        code_choice.reshape(1, -1),
    )
    mixed = grouped_conv(
        windows.reshape(dps * utts, 3 * frames, LANES), taps.reshape(-1, inner, inner)
    )

    all_codes = codes.reshape(seqs * frames, code_choice.shape[-1])
    all_targets = make_targets(all_codes, codebook, quant_weight)
    wide_targets = all_targets.astype(jnp.float32)
    tgt_norm = jnp.sum(wide_targets * wide_targets, axis=-1)[None, :]
    own_targets = lax.dynamic_slice_in_dim(
        all_targets, lax.axis_index("seq") * frames, frames, 0
    )
    ids = negative_ids.reshape(frames, negative_ids.shape[-1])
    frame_row = jnp.arange(seqs * frames, dtype=jnp.int32)
    counts = jnp.sum((ids[:, :, None] == frame_row).astype(jnp.float32), axis=1)
    own_masked = lax.dynamic_slice_in_dim(
        masked, lax.axis_index("tensor") * frames, frames, 0
    )
    loss = back(
        sizes,
        mixed,
        final_weight.reshape(groups, inner, final_weight.shape[1]),
        all_targets,
        own_targets,
        tgt_norm,
        counts,
        own_masked,
    )
    return loss.reshape(1, frames)


def solution(mesh):
    return jax.shard_map(
        on_device,
        mesh=mesh,
        in_specs=(
            P("dp", "seq", "tensor"),
            P(None, "tensor", None),
            P(None, "tensor"),
            P("tensor"),
            P(("dp", "seq"), "tensor", None, None),
            P("tensor", None),
            P(),
            P(),
            P("dp", None),
            P(("dp", "tensor"), "seq", None),
            P(("dp", "tensor"), "seq", None),
        ),
        out_specs=P(("dp", "tensor"), "seq"),
        check_vma=False,
    )
```

time: 170 us -> 96.4 us (0.57)
  waiting for transfers between devices: 74.7 us -> 0 us
  Pallas kernels: 20.6 us -> 73.7 us
  blocking collectives: 21.2 us -> 0 us
  between operations: 15.1 us -> 0.24 us
  starting transfers between devices: 7.11 us -> 0 us
  matrix products: 9.99 us -> 6.54 us
  other arithmetic: 8.87 us -> 5.57 us
    pallas_call x2 -> x3, Pallas kernels: 20.6 us -> 73.7 us  [the longest x1 43 us: front(): pl.pallas_call(functools.partial(front_body, sizes), out_shape=(jax.Shape...]
    all_gather x1 -> x0, waiting for transfers between devices: 27.1 us -> none  [on_device(): taps = lax.all_gather(pos_weight, ('dp', 'seq'), axis=0, tiled=True)]
    reduce_scatter x1 -> x0, waiting for transfers between devices: 21.9 us -> none  [on_device(): lax.psum_scatter(partial, 'tensor', scatter_dimension=0, tiled=True)]
    all_gather x1 -> x0, blocking collectives: 21.2 us -> none  [on_device(): lax.all_gather(code_choice.reshape(-1), 'seq', axis=0, tiled=True)]
    psum x1 -> x0, waiting for transfers between devices: 19.9 us -> none  [on_device(): summed = lax.psum(conv_term, 'tensor')]
    ppermute x2 -> x0, starting transfers between devices: 6.99 us -> none  [the longest x1 5.07 us: extended(): lax.ppermute(lax.slice_in_dim(block, block.shape[dim] - width, None, axis...]
    ppermute x2 -> x0, waiting for transfers between devices: 5.28 us -> none  [the longest x1 3.49 us: extended(): lax.ppermute(lax.slice_in_dim(block, 0, width, axis=dim), axis, backward)]
    dot_general x2 -> x0, matrix products: 4.45 us -> none  [the longest x1 2.45 us: on_device(): jnp.dot(features, proj_weight, preferred_element_type=jnp.float32)]
  transfers between devices with their start and end apart: 5 -> 0, of which waited for: 5 -> 0; matrix products, arithmetic and copies ran while one was open for 13% -> 0% of each run, Pallas kernels for 0% -> 0%
where the time goes in v2:
time: 96.4 us; the launch traced here: 96.1 us
  Pallas kernels  73.7 us (76%)
  local copies, waits for them, and re-layouts  10.1 us (10%)
  matrix products  6.54 us (7%)
  other arithmetic  5.57 us (6%)
    pallas_call x1, Pallas kernels, front(): pl.pallas_call(functools.partial(front_body, sizes), out_shape=(jax.Shape...  43 us
    pallas_call x1, Pallas kernels, back(): pl.pallas_call(functools.partial(back_body, sizes), out_shape=jax.ShapeDt...  18.6 us
    pallas_call x1, Pallas kernels, grouped_conv(): pl.pallas_call(conv_body, grid=(steps,), out_shape=jax.ShapeDtypeStruct((...  12 us
    reduce_sum x1, other arithmetic, on_device(): counts = jnp.sum((ids[:, :, None] == frame_row).astype(jnp.float32), axis=1)  4.04 us
    dot_general x1, matrix products, make_targets(): jnp.dot(codevec, quant_weight, preferred_element_type=jnp.float32)  3.8 us
    unnamed x21, local copies, waits for them, and re-layouts  2.92 us
    dot_general x2, matrix products, make_targets(): jnp.dot(onehot, codebook[qgroup], preferred_element_type=jnp.float32)  2.74 us
    reshape x1, local copies, waits for them, and re-layouts, on_device(): proj_weight.reshape(proj_weight.shape[0], groups, inner).transpose(1, 0, 2)  2.03 us

profile of v2, /device:TPU:1, one launch (start us, length us, event | category | flops | bytes accessed | tf_op | source)
XLA Modules:
  0.0 96.1 jit_solution(16816238295012155796)
XLA Ops:
  0.0 0.0 copy-start
  0.0 0.0 copy-start.6
  0.0 0.0 copy-start.4
  0.0 1.1 %reshape.51.pairs_ref = bf16[256,256]{1,0:T(8,128)(2,1)S(1)} reshape(bf16[4,128,128]{2,1,0:T(8,128)(2,1)} %param.11) | data formatting | bytes 262144 | tf_op jit(solution)/shard_map/reshape | solution.py:522
  1.1 2.0 %copy.18 = bf16[512,4,120]{2,0,1:T(8,128)(2,1)} copy(bf16[512,4,120]{0,2,1:T(8,128)(2,1)} %bitcast.22) | data formatting | bytes 983040 | tf_op jit(solution)/shard_map/reshape | solution.py:524
  3.2 1.1 %pad.8.pw_ref = bf16[4,512,128]{2,1,0:T(8,128)(2,1)S(1)} pad(bf16[4,512,120]{2,1,0:T(8,128)(2,1)} %bitcast.21, bf16[]{:T(256)} %constant.4.clone.1), padding=0_0x0_0x0_8 | pad | bytes 1015810 | tf_op jit(solution)/shard_map/jit(_pad)/pad | solution.py:525
  4.3 0.1 reshape.62
  4.4 0.0 copy-done.6
  4.5 0.2 and_reduce_fusion
  4.7 0.1 reshape.63.mask_ref
  4.9 0.1 copy.20
  4.9 0.1 reshape.55.codes_in
  5.1 43.0 %shard_map.109 = (bf16[16,3,64,128]{3,2,1,0:T(8,128)(2,1)S(1)}, bf16[4,16,2,120,120]{4,3,2,1,0:T(8,128)(2,1)S(1)}, s32[16,1,128]{2,1,0:T(1,128)S(1)}) custom-call(bf16[256,256]{1,0:T(8,128)(2,1)S(1)} %reshape.51.pairs_ref, bf16[256,512]{1,0:T(8,128)(2,1)S(1)} %bitcast.19, bf16[4,512,128]{2,1,0:T(8,128)(2,1)S(1)} %pad.8.pw_ref, ...), custom_call_target="tpu_custom_call" | custom-call | tf_op jit(solution)/shard_map/pallas_call | solution.py:285
  48.2 12.0 %shard_map.110.mixed_ref = bf16[16,64,128]{2,1,0:T(8,128)(2,1)S(1)} custom-call(bf16[16,192,128]{2,1,0:T(8,128)(2,1)S(1)} %bitcast.18, bf16[128,120,120]{2,1,0:T(8,128)(2,1)S(1)} %bitcast.16), custom_call_target="tpu_custom_call" | custom-call | tf_op jit(solution)/shard_map/pallas_call | solution.py:372
  60.2 0.5 broadcast.17
  60.7 0.7 reduce.8
  61.4 0.5 reshape.59
  61.9 0.0 copy-start.9
  61.9 0.5 slice_reduce_fusion.1
  62.4 1.9 %fusion.9 = bf16[1024,512]{0,1:T(8,128)(2,1)S(1)} fusion(s32[1024]{0:T(1024)S(1)} %get-tuple-element.12, bf16[2,320,512]{2,1,0:T(8,128)(2,1)} %param.17), kind=kOutput, calls=%fused_computation.12 | convolution fusion | flops 336396288 | bytes 1380352 | tf_op jit(solution)/shard_map/dot_general | solution.py:32
  64.2 0.0 copy-done.9
  64.3 0.9 fusion.10
  65.2 0.0 copy-done
  65.2 0.0 copy-start.5
  65.2 3.8 %multiply_reduce_fusion = (f32[1024]{0:T(1024)S(1)}, bf16[1024,1024]{1,0:T(8,128)(2,1)}) fusion(bf16[1024,1024]{1,0:T(8,128)(2,1)S(1)} %copy-done, bf16[1024,512]{0,1:T(8,128)(2,1)S(1)} %fusion.9, bf16[1024,512]{0,1:T(8,128)(2,1)S(1)} %fusion.10), kind=kOutput, calls=%fused_computation.2 | convolution fusion | flops 2155871232 | bytes 6295552 | tf_op jit(solution)/shard_map/dot_general | solution.py:37
  69.0 0.9 constant_dynamic-slice_fusion.1.own_ref
  69.9 0.1 copy.22
  70.0 4.0 %convert_reduce_fusion.count_ref = f32[64,1024]{1,0:T(8,128)S(1)} fusion(s32[64,100]{0,1:T(8,128)S(1)} %copy.22), kind=kLoop, calls=%fused_computation | loop fusion | flops 19595264 | bytes 287744 | tf_op jit(solution)/shard_map/reduce_sum | solution.py:558
  74.1 1.6 %copy-done.1 = bf16[1024,1024]{1,0:T(8,128)(2,1)S(1)} copy-done((bf16[1024,1024]{1,0:T(8,128)(2,1)S(1)}, bf16[1024,1024]{1,0:T(8,128)(2,1)}, u32[]{:S(2)}) %copy-start.1) | copy-done | bytes 2097176
  75.7 1.2 %copy-done.2 = bf16[480,1024]{1,0:T(8,128)(2,1)S(1)} copy-done((bf16[480,1024]{1,0:T(8,128)(2,1)S(1)}, bf16[480,1024]{1,0:T(8,128)(2,1)}, u32[]{:S(2)}) %copy-start.2) | copy-done | bytes 983064
  76.9 18.6 %shard_map.111 = f32[64,1]{1,0:T(8,128)S(1)} custom-call(bf16[16,64,128]{2,1,0:T(8,128)(2,1)S(1)} %shard_map.110.mixed_ref, bf16[4,120,1024]{2,1,0:T(8,128)(2,1)S(1)} %bitcast.17, bf16[1024,1024]{1,0:T(8,128)(2,1)S(1)} %copy-done.1, bf16[64,1024]{1,0:T(8,128)(2,1)S(1)} %constant_dynamic-slice_fusion.1.own_ref, f32[1,1024]{1,0:T(1,128)S(1)} %bitcast.20, ...), custom_call_target="tpu_custom_call" | custom-call | tf_op jit(solution)/shard_map/pallas_call | solution.py:481
  95.5 0.6 reduce.3
  (15 shorter events, 0.1 us)
Async XLA Ops:
  0.0 65.2 %copy-start = (bf16[1024,1024]{1,0:T(8,128)(2,1)S(1)}, bf16[1024,1024]{1,0:T(8,128)(2,1)}, u32[]{:S(2)}) copy-start(bf16[1024,1024]{1,0:T(8,128)(2,1)} %param.18) | copy-start | bytes 6291460
  0.0 5.1 %copy-start.3 = (bf16[2,128,512]{2,1,0:T(8,128)(2,1)S(1)}, bf16[2,128,512]{2,1,0:T(8,128)(2,1)}, u32[]{:S(2)}) copy-start(bf16[2,128,512]{2,1,0:T(8,128)(2,1)} %param.12) | copy-start | bytes 786436
  0.0 4.3 %copy-start.7 = (bf16[480]{0:T(512)(128)(2,1)S(1)}, bf16[480]{0:T(512)(128)(2,1)}, u32[]{:S(2)}) copy-start(bf16[480]{0:T(512)(128)(2,1)} %param.14) | copy-start | bytes 2884
  0.0 4.4 %copy-start.6 = (s32[4,66]{1,0:T(4,128)S(1)}, s32[4,66]{1,0:T(4,128)}, u32[]{:S(2)}) copy-start(s32[4,66]{1,0:T(4,128)} %param.19) | copy-start | bytes 3172
  0.0 5.1 %copy-start.4 = (bf16[2,4,120,120]{3,2,1,0:T(8,128)(2,1)S(1)}, bf16[2,4,120,120]{3,2,1,0:T(8,128)(2,1)}, u32[]{:S(2)}) copy-start(bf16[2,4,120,120]{3,2,1,0:T(8,128)(2,1)} %taps_in.1) | copy-start | bytes 691204
  0.0 4.8 %copy-start.8 = (s32[1,64,2]{1,2,0:T(2,128)S(1)}, s32[1,64,2]{1,2,0:T(2,128)}, u32[]{:S(2)}) copy-start(s32[1,64,2]{1,2,0:T(2,128)} %param.20) | copy-start | bytes 1540
  61.9 2.4 %copy-start.9 = (bf16[2,320,512]{2,1,0:T(8,128)(2,1)S(1)}, bf16[2,320,512]{2,1,0:T(8,128)(2,1)}, u32[]{:S(2)}) copy-start(bf16[2,320,512]{2,1,0:T(8,128)(2,1)} %param.17) | copy-start | bytes 1966084
  65.2 4.7 %copy-start.5 = (s32[1,64,100]{2,1,0:T(8,128)S(1)}, s32[1,64,100]{2,1,0:T(8,128)}, u32[]{:S(2)}) copy-start(s32[1,64,100]{2,1,0:T(8,128)} %param.21) | copy-start | bytes 76804
  74.1 1.6 %copy-start.1 = (bf16[1024,1024]{1,0:T(8,128)(2,1)S(1)}, bf16[1024,1024]{1,0:T(8,128)(2,1)}, u32[]{:S(2)}) copy-start(bf16[1024,1024]{1,0:T(8,128)(2,1)} %get-tuple-element.14.t_ref) | copy-start | bytes 6291460
  75.7 1.2 %copy-start.2 = (bf16[480,1024]{1,0:T(8,128)(2,1)S(1)}, bf16[480,1024]{1,0:T(8,128)(2,1)}, u32[]{:S(2)}) copy-start(bf16[480,1024]{1,0:T(8,128)(2,1)} %param.16) | copy-start | bytes 2949124

commit v3 on v2

--- a/solution.py
+++ b/solution.py
@@ -20,21 +20,6 @@
 
 def exact_gelu(value):
     return 0.5 * value * (1.0 + lax.erf(value * (0.5**0.5)))
-
-
-def make_targets(code_block, codebook, quant_weight):
-    entries = codebook.shape[1]
-    choices_row = jnp.arange(entries, dtype=jnp.int32)
-    pieces = []
-    for qgroup in range(codebook.shape[0]):
-        onehot = (code_block[..., qgroup, None] == choices_row).astype(jnp.bfloat16)
-        pieces.append(
-            jnp.dot(onehot, codebook[qgroup], preferred_element_type=jnp.float32).astype(
-                jnp.bfloat16
-            )
-        )
-    codevec = jnp.concatenate(pieces, axis=-1)
-    return jnp.dot(codevec, quant_weight, preferred_element_type=jnp.float32).astype(jnp.bfloat16)
 
 
 def remote(src, dst, send, recv, **coords):
@@ -63,9 +48,15 @@
     mask_ref,
     taps_in,
     codes_in,
+    book_ref,
+    qw_ref,
     win_ref,
     taps_ref,
+    targets_ref,
+    norms_ref,
     codes_ref,
+    choice,
+    codevec,
     term_wide,
     term_half,
     arrived,
@@ -230,10 +221,17 @@
         copy.wait_recv()
     features = feat[...].reshape(utts * frames, channels)
     is_masked = mask_ref[...] > 0
+    inner = embed_ref.shape[-1]
+    hidden[...] = jnp.zeros_like(hidden)
     for group in range(dps):
-        projected = jnp.dot(features, pw_ref[group], preferred_element_type=jnp.float32)
+        projected = lax.dot_general(
+            features,
+            pw_ref[group * inner : (group + 1) * inner, :],
+            (((1,), (1,)), ((), ())),
+            preferred_element_type=jnp.float32,
+        )
         chosen = jnp.where(is_masked, embed_ref[group].astype(jnp.float32), projected)
-        hidden[group] = chosen.astype(jnp.bfloat16).reshape(utts, frames, LANES)
+        hidden[group, :, :, :inner] = chosen.astype(jnp.bfloat16).reshape(utts, frames, inner)
     mine = pl.ds(dp * utts, utts)
     win_copies = []
     for k in range(dps):
@@ -254,7 +252,34 @@
                 )
             )
     win_ref[mine, 1] = hidden[dp]
+    for copy in code_copies:
+        copy.wait_recv()
+    for block in range(seqs):
+        choice[:, block * frames : (block + 1) * frames] = codes_ref[block]
+    entries, width = book_ref.shape[1:]
+    half = choice.shape[1] // 2
+
+    def make_targets(part):
+        here = slice(part * half, (part + 1) * half)
+        for qgroup in range(book_ref.shape[0]):
+            row = lax.broadcasted_iota(jnp.int32, (entries, half), 0)
+            onehot = jnp.where(row == choice[qgroup : qgroup + 1, here], 1.0, 0.0)
+            codevec[:, qgroup * width : (qgroup + 1) * width] = lax.dot_general(
+                onehot.astype(jnp.bfloat16),
+                book_ref[qgroup],
+                (((0,), (0,)), ((), ())),
+                preferred_element_type=jnp.float32,
+            ).astype(jnp.bfloat16)
+        made = jnp.dot(codevec[...], qw_ref[...], preferred_element_type=jnp.float32)
+        made = made.astype(jnp.bfloat16)
+        targets_ref[here, :] = made
+        made = made.astype(jnp.float32)
+        norm = jnp.sum(made * made, axis=-1, keepdims=True)
+        norms_ref[:, here] = jnp.transpose(jnp.broadcast_to(norm, (half, LANES)))[:1]
+
+    make_targets(0)
     advance(2)
+    make_targets(1)
     for copy in win_copies:
         copy.wait_recv()
 
@@ -268,13 +293,13 @@
 
     for step in range(3, ups + 1):
         advance(step)
-    for copy in pair_copies + code_copies:
+    for copy in pair_copies:
         copy.wait_recv()
     for copy in pending:
         copy.wait_send()
 
 
-def front(sizes, utts, pairs, cw, pw, embed, mask, taps, codes):
+def front(sizes, utts, pairs, cw, pw, embed, mask, taps, codes, book, qw):
     dps, seqs, tensors = sizes
     frames = mask.shape[0] // utts
     channels = cw.shape[1]
@@ -287,11 +312,15 @@
         out_shape=(
             jax.ShapeDtypeStruct((utts * dps, 3, frames, LANES), jnp.bfloat16),
             jax.ShapeDtypeStruct((dps, seqs, per, inner, outer), jnp.bfloat16),
-            jax.ShapeDtypeStruct((seqs,) + codes.shape, codes.dtype),
+            jax.ShapeDtypeStruct((seqs * frames, qw.shape[1]), jnp.bfloat16),
+            jax.ShapeDtypeStruct((1, seqs * frames), jnp.float32),
         ),
-        in_specs=[vmem] * 7,
-        out_specs=(vmem, pl.BlockSpec(memory_space=pl.ANY), vmem),
+        in_specs=[vmem] * 9,
+        out_specs=(vmem, pl.BlockSpec(memory_space=pl.ANY), vmem, vmem),
         scratch_shapes=[
+            pltpu.VMEM((seqs,) + codes.shape, codes.dtype),
+            pltpu.VMEM((codes.shape[0], seqs * frames), codes.dtype),
+            pltpu.VMEM((seqs * frames // 2, qw.shape[0]), jnp.bfloat16),
             pltpu.VMEM((utts, frames, channels), jnp.float32),
             pltpu.VMEM((utts, frames, channels), jnp.bfloat16),
             pltpu.VMEM((tensors - 1, frames, channels), jnp.bfloat16),
@@ -316,7 +345,7 @@
         compiler_params=pltpu.CompilerParams(
             collective_id=0, has_side_effects=True, vmem_limit_bytes=40 * 2**20
         ),
-    )(pairs, cw, pw, embed, mask, taps, codes)
+    )(pairs, cw, pw, embed, mask, taps, codes, book, qw)
 
 
 def conv_body(x_ref, w_ref, o_ref, xf, xc, wc, acc):
@@ -392,14 +421,8 @@
     sizes,
     mixed_ref,
     fw_ref,
-    t_ref,
-    own_ref,
-    tn_ref,
-    count_ref,
-    mask_ref,
     o_ref,
     gathered,
-    part_wide,
     part_half,
     arrived,
     mix_send,
@@ -409,7 +432,8 @@
 ):
     dps, _, tensors = sizes
     dp, tensor = lax.axis_index("dp"), lax.axis_index("tensor")
-    utts, frames, code_dim = part_wide.shape
+    _, utts, frames, _ = gathered.shape
+    code_dim = o_ref.shape[1]
     inner = fw_ref.shape[1]
 
     barrier = pltpu.get_barrier_semaphore()
@@ -455,37 +479,23 @@
     for k, copy in enumerate(sum_copies):
         copy.wait_recv()
         total += arrived[k].astype(jnp.float32)
-    context = total.astype(jnp.bfloat16)
-    scores = lax.dot_general(
-        context, t_ref[...], (((1,), (1,)), ((), ())), preferred_element_type=jnp.float32
-    )
-    wide = context.astype(jnp.float32)
-    own = own_ref[...].astype(jnp.float32)
-    ctx_norm = jnp.sum(wide * wide, axis=-1, keepdims=True) + norm_eps
-    own_norm = jnp.sum(own * own, axis=-1, keepdims=True) + norm_eps
-    pos_dot = jnp.sum(wide * own, axis=-1, keepdims=True)
-    positive = pos_dot * lax.rsqrt(ctx_norm * own_norm) / logit_temp
-    logits = scores * lax.rsqrt(ctx_norm * (tn_ref[...] + norm_eps)) / logit_temp
-    negatives = jnp.sum(count_ref[...] * jnp.exp(logits), axis=-1, keepdims=True)
-    loss = jnp.log(jnp.exp(positive) + negatives) - positive
-    o_ref[...] = jnp.where(mask_ref[...] > 0, loss, 0.0)
+    o_ref[...] = total.astype(jnp.bfloat16)
     for copy in mix_copies + sum_copies:
         copy.wait_send()
 
 
-def back(sizes, mixed, fw, targets, own, norms, counts, mask):
+def back(sizes, mixed, fw):
     dps, _, tensors = sizes
     utts, frames = mixed.shape[0] // dps, mixed.shape[1]
     code_dim = fw.shape[-1]
     dma = pltpu.SemaphoreType.DMA
     return pl.pallas_call(
         functools.partial(back_body, sizes),
-        out_shape=jax.ShapeDtypeStruct((frames, 1), jnp.float32),
-        in_specs=[pl.BlockSpec(memory_space=pltpu.VMEM)] * 7,
+        out_shape=jax.ShapeDtypeStruct((frames, code_dim), jnp.bfloat16),
+        in_specs=[pl.BlockSpec(memory_space=pltpu.VMEM)] * 2,
         out_specs=pl.BlockSpec(memory_space=pltpu.VMEM),
         scratch_shapes=[
             pltpu.VMEM((dps, utts, frames, LANES), jnp.bfloat16),
-            pltpu.VMEM((utts, frames, code_dim), jnp.float32),
             pltpu.VMEM((tensors - 1, frames, code_dim), jnp.bfloat16),
             pltpu.VMEM((tensors - 1, frames, code_dim), jnp.bfloat16),
             dma((dps - 1,)),
@@ -496,7 +506,48 @@
         compiler_params=pltpu.CompilerParams(
             collective_id=1, has_side_effects=True, vmem_limit_bytes=32 * 2**20
         ),
-    )(mixed, fw, targets, own, norms, counts, mask)
+    )(mixed, fw)
+
+
+def loss_body(c_ref, t_ref, tn_ref, ids_ref, mask_ref, o_ref, ids):
+    context = c_ref[...]
+    frames, negs = ids_ref.shape
+    ids[...] = jnp.zeros_like(ids)
+    ids[:, :negs] = ids_ref[...]
+    first = pl.multiple_of(lax.axis_index("seq") * frames, frames)
+    scores = lax.dot_general(
+        context, t_ref[...], (((1,), (1,)), ((), ())), preferred_element_type=jnp.float32
+    )
+    wide = context.astype(jnp.float32)
+    own = t_ref[pl.ds(first, frames), :].astype(jnp.float32)
+    ctx_norm = jnp.sum(wide * wide, axis=-1, keepdims=True) + norm_eps
+    own_norm = jnp.sum(own * own, axis=-1, keepdims=True) + norm_eps
+    pos_dot = jnp.sum(wide * own, axis=-1, keepdims=True)
+    positive = pos_dot * lax.rsqrt(ctx_norm * own_norm) / logit_temp
+    logits = scores * lax.rsqrt(ctx_norm * (tn_ref[...] + norm_eps)) / logit_temp
+    powers = jnp.exp(logits)
+    chosen = ids[...]
+    lane = chosen % LANES
+    chunk = chosen // LANES
+    picked = jnp.zeros((frames, LANES), jnp.float32)
+    for c in range(powers.shape[1] // LANES):
+        found = jnp.take_along_axis(
+            powers[:, c * LANES : (c + 1) * LANES], lane, axis=1, mode="promise_in_bounds"
+        )
+        picked = jnp.where(chunk == c, found, picked)
+    real = lax.broadcasted_iota(jnp.int32, picked.shape, 1) < negs
+    negatives = jnp.sum(jnp.where(real, picked, 0.0), axis=-1, keepdims=True)
+    loss = jnp.log(jnp.exp(positive) + negatives) - positive
+    o_ref[...] = jnp.where(mask_ref[...] > 0, loss, 0.0)
+
+
+def losses(context, targets, norms, ids, mask):
+    return pl.pallas_call(
+        loss_body,
+        out_shape=jax.ShapeDtypeStruct((ids.shape[0], 1), jnp.float32),
+        scratch_shapes=[pltpu.VMEM((ids.shape[0], LANES), jnp.int32)],
+        compiler_params=pltpu.CompilerParams(vmem_limit_bytes=24 * 2**20),
+    )(context, targets, norms, ids, mask)
 
 
 def on_device(
@@ -517,13 +568,10 @@
     sizes = tuple(lax.axis_size(name) for name in ("dp", "seq", "tensor"))
     dps, seqs, tensors = sizes
     groups, inner = pos_weight.shape[1], pos_weight.shape[2]
-    padding = LANES - inner
 
     pairs = feature_in.reshape(utts * frames, 2 * channels)
     cw = conv_weight.reshape(2 * channels, conv_weight.shape[2])
-    pw = proj_weight.reshape(proj_weight.shape[0], groups, inner).transpose(1, 0, 2)
-    pw = jnp.pad(pw, ((0, 0), (0, 0), (0, padding)))
-    embed = jnp.pad(mask_embed.reshape(groups, 1, inner), ((0, 0), (0, 0), (0, padding)))
+    embed = mask_embed.reshape(groups, 1, inner)
     positions = (lax.axis_index("seq") * frames + jnp.arange(frames, dtype=jnp.int32))[
         None, :, None
     ]
@@ -531,44 +579,27 @@
     masked = jnp.any((positions >= starts) & (positions < starts + MASK_LEN), axis=-1)
     masked = masked.astype(jnp.float32).reshape(utts * frames, 1)
 
-    windows, taps, codes = front(
+    windows, taps, targets, norms = front(
         sizes,
         utts,
         pairs,
         cw,
-        pw,
+        proj_weight.T,
         embed,
         masked,
         pos_weight,
-        code_choice.reshape(1, -1),
+        code_choice[0].T,
+        codebook,
+        quant_weight,
     )
     mixed = grouped_conv(
         windows.reshape(dps * utts, 3 * frames, LANES), taps.reshape(-1, inner, inner)
     )
-
-    all_codes = codes.reshape(seqs * frames, code_choice.shape[-1])
-    all_targets = make_targets(all_codes, codebook, quant_weight)
-    wide_targets = all_targets.astype(jnp.float32)
-    tgt_norm = jnp.sum(wide_targets * wide_targets, axis=-1)[None, :]
-    own_targets = lax.dynamic_slice_in_dim(
-        all_targets, lax.axis_index("seq") * frames, frames, 0
-    )
-    ids = negative_ids.reshape(frames, negative_ids.shape[-1])
-    frame_row = jnp.arange(seqs * frames, dtype=jnp.int32)
-    counts = jnp.sum((ids[:, :, None] == frame_row).astype(jnp.float32), axis=1)
+    context = back(sizes, mixed, final_weight.reshape(groups, inner, final_weight.shape[1]))
     own_masked = lax.dynamic_slice_in_dim(
         masked, lax.axis_index("tensor") * frames, frames, 0
     )
-    loss = back(
-        sizes,
-        mixed,
-        final_weight.reshape(groups, inner, final_weight.shape[1]),
-        all_targets,
-        own_targets,
-        tgt_norm,
-        counts,
-        own_masked,
-    )
+    loss = losses(context, targets, norms, negative_ids[0], own_masked)
     return loss.reshape(1, frames)
 
 

time: 96.4 us -> 84.5 us (0.88)
  matrix products: 6.54 us -> 0 us
  other arithmetic: 5.57 us -> 2.22 us
  local copies, waits for them, and re-layouts: 10.1 us -> 8.15 us
    dot_general x3 -> x0, matrix products: 6.54 us -> none  [the longest x1 3.8 us: make_targets(): jnp.dot(codevec, quant_weight, preferred_element_type=jnp.float32)]
    reduce_sum x1 -> x0, other arithmetic: 4.04 us -> none  [on_device(): counts = jnp.sum((ids[:, :, None] == frame_row).astype(jnp.float32), axis=1)]
    unnamed x21 -> x16, local copies, waits for them, and re-layouts: 2.92 us -> 6.29 us
    reshape x4 -> x1, local copies, waits for them, and re-layouts: 2.72 us -> 0.76 us  [on_device(): embed = mask_embed.reshape(groups, 1, inner)]
    pad x2 -> x0, local copies, waits for them, and re-layouts: 1.16 us -> none  [the longest x1 1.15 us: on_device(): pw = jnp.pad(pw, ((0, 0), (0, 0), (0, padding)))]
    pallas_call x0 -> x1, Pallas kernels: none -> 0.97 us  [losses(): pl.pallas_call(loss_body, out_shape=jax.ShapeDtypeStruct((ids.shape[0], 1...]
where the time goes in v3:
time: 84.5 us; the launch traced here: 84.2 us
  Pallas kernels  73.7 us (87%)
  local copies, waits for them, and re-layouts  8.15 us (10%)
  other arithmetic  2.22 us (3%)
    pallas_call x1, Pallas kernels, front(): pl.pallas_call(functools.partial(front_body, sizes), out_shape=(jax.Shape...  42.8 us
    pallas_call x1, Pallas kernels, back(): pl.pallas_call(functools.partial(back_body, sizes), out_shape=jax.ShapeDt...  17.9 us
    pallas_call x1, Pallas kernels, grouped_conv(): pl.pallas_call(conv_body, grid=(steps,), out_shape=jax.ShapeDtypeStruct((...  12.1 us
    unnamed x16, local copies, waits for them, and re-layouts  6.29 us

profile of v3, /device:TPU:1, one launch (start us, length us, event | category | flops | bytes accessed | tf_op | source)
XLA Modules:
  0.0 84.2 jit_solution(9290947431272007527)
XLA Ops:
  0.0 0.8 reshape.49.embed_ref
  0.8 0.7 broadcast_add_fusion
  1.5 0.9 %and_reduce_fusion = pred[4,64]{1,0:T(4,128)(4,1)S(1)} fusion(s32[4,66]{1,0:T(4,128)S(1)} %broadcast_add_fusion, s32[4,66]{1,0:T(4,128)} %param.19, s32[64]{0:T(128)S(1)} %iota_add_fusion), kind=kLoop, calls=%fused_computation | loop fusion | flops 67328 | bytes 2624 | tf_op jit(solution)/shard_map/reduce_or | solution.py:579
  2.4 0.1 reshape.50.mask_ref
  2.5 1.0 %reshape.41.pairs_ref = bf16[256,256]{1,0:T(8,128)(2,1)S(1)} reshape(bf16[4,128,128]{2,1,0:T(8,128)(2,1)} %param.11) | data formatting | bytes 262144 | tf_op jit(solution)/shard_map/reshape | solution.py:572
  3.5 0.0 copy-start
  3.5 1.6 %copy-done = bf16[1024,1024]{1,0:T(8,128)(2,1)S(1)} copy-done((bf16[1024,1024]{1,0:T(8,128)(2,1)S(1)}, bf16[1024,1024]{1,0:T(8,128)(2,1)}, u32[]{:S(2)}) %copy-start) | copy-done | bytes 2097176
  5.1 0.0 copy-start.2
  5.1 1.1 %copy-done.2 = bf16[2,320,512]{2,1,0:T(8,128)(2,1)S(1)} copy-done((bf16[2,320,512]{2,1,0:T(8,128)(2,1)S(1)}, bf16[2,320,512]{2,1,0:T(8,128)(2,1)}, u32[]{:S(2)}) %copy-start.2) | copy-done | bytes 655384
  6.2 0.0 copy-start.3
  6.2 1.0 %copy-done.3 = bf16[512,480]{0,1:T(8,128)(2,1)S(1)} copy-done((bf16[512,480]{0,1:T(8,128)(2,1)S(1)}, bf16[512,480]{0,1:T(8,128)(2,1)}, u32[]{:S(2)}) %copy-start.3) | copy-done | bytes 491544
  7.2 0.0 copy-start.4
  7.2 0.9 %copy-done.4 = bf16[2,128,512]{2,1,0:T(8,128)(2,1)S(1)} copy-done((bf16[2,128,512]{2,1,0:T(8,128)(2,1)S(1)}, bf16[2,128,512]{2,1,0:T(8,128)(2,1)}, u32[]{:S(2)}) %copy-start.4) | copy-done | bytes 262168
  8.1 0.0 copy-start.5
  8.2 0.9 %copy-done.5 = bf16[2,4,120,120]{3,2,1,0:T(8,128)(2,1)S(1)} copy-done((bf16[2,4,120,120]{3,2,1,0:T(8,128)(2,1)S(1)}, bf16[2,4,120,120]{3,2,1,0:T(8,128)(2,1)}, u32[]{:S(2)}) %copy-start.5) | copy-done | bytes 230424
  9.1 0.0 copy-start.7
  9.1 0.7 copy-done.7
  9.8 42.8 %shard_map.109 = (bf16[16,3,64,128]{3,2,1,0:T(8,128)(2,1)S(1)}, bf16[4,16,2,120,120]{4,3,2,1,0:T(8,128)(2,1)S(1)}, bf16[1024,1024]{1,0:T(8,128)(2,1)S(1)}, f32[1,1024]{1,0:T(1,128)S(1)}) custom-call(bf16[256,256]{1,0:T(8,128)(2,1)S(1)} %reshape.41.pairs_ref, bf16[256,512]{1,0:T(8,128)(2,1)S(1)} %bitcast.14, bf16[480,512]{1,0:T(8,128)(2,1)S(1)} %bitcast.13, ...), custom_call_target="tpu_custom_call" | custom-call | tf_op jit(solution)/shard_map/pallas_call | solution.py:310
  52.6 0.0 copy-start.1
  52.6 0.0 copy-start.6
  52.6 12.1 %shard_map.110.mixed_ref = bf16[16,64,128]{2,1,0:T(8,128)(2,1)S(1)} custom-call(bf16[16,192,128]{2,1,0:T(8,128)(2,1)S(1)} %bitcast.12, bf16[128,120,120]{2,1,0:T(8,128)(2,1)S(1)} %bitcast.10), custom_call_target="tpu_custom_call" | custom-call | tf_op jit(solution)/shard_map/pallas_call | solution.py:401
  64.6 0.0 copy-done.1
  64.6 17.9 %shard_map.111.c_ref = bf16[64,1024]{1,0:T(8,128)(2,1)S(1)} custom-call(bf16[16,64,128]{2,1,0:T(8,128)(2,1)S(1)} %shard_map.110.mixed_ref, bf16[4,120,1024]{2,1,0:T(8,128)(2,1)S(1)} %bitcast.11), custom_call_target="tpu_custom_call" | custom-call | tf_op jit(solution)/shard_map/pallas_call | solution.py:492
  82.6 0.0 copy-done.6
  82.6 1.0 %shard_map.112 = f32[64,1]{1,0:T(8,128)S(1)} custom-call(bf16[64,1024]{1,0:T(8,128)(2,1)S(1)} %shard_map.111.c_ref, bf16[1024,1024]{1,0:T(8,128)(2,1)S(1)} %get-tuple-element.11.t_ref, f32[1,1024]{1,0:T(1,128)S(1)} %get-tuple-element.12.tn_ref, s32[64,100]{1,0:T(8,128)S(1)} %bitcast.15, f32[64,1]{1,0:T(8,128)S(1)} %constant_dynamic-slice_fusion.mask_ref), custom_call_target="tpu_custom_call" | custom-call | tf_op jit(solution)/shard_map/pallas_call | solution.py:545
  83.5 0.6 reduce
  (3 shorter events, 0.0 us)
Async XLA Ops:
  3.5 1.6 %copy-start = (bf16[1024,1024]{1,0:T(8,128)(2,1)S(1)}, bf16[1024,1024]{1,0:T(8,128)(2,1)}, u32[]{:S(2)}) copy-start(bf16[1024,1024]{1,0:T(8,128)(2,1)} %qw_ref.1) | copy-start | bytes 6291460
  5.1 1.1 %copy-start.2 = (bf16[2,320,512]{2,1,0:T(8,128)(2,1)S(1)}, bf16[2,320,512]{2,1,0:T(8,128)(2,1)}, u32[]{:S(2)}) copy-start(bf16[2,320,512]{2,1,0:T(8,128)(2,1)} %book_ref.1) | copy-start | bytes 1966084
  6.2 1.0 %copy-start.3 = (bf16[512,480]{0,1:T(8,128)(2,1)S(1)}, bf16[512,480]{0,1:T(8,128)(2,1)}, u32[]{:S(2)}) copy-start(bf16[512,480]{0,1:T(8,128)(2,1)} %param.13) | copy-start | bytes 1474564
  7.2 0.9 %copy-start.4 = (bf16[2,128,512]{2,1,0:T(8,128)(2,1)S(1)}, bf16[2,128,512]{2,1,0:T(8,128)(2,1)}, u32[]{:S(2)}) copy-start(bf16[2,128,512]{2,1,0:T(8,128)(2,1)} %param.12) | copy-start | bytes 786436
  8.1 0.9 %copy-start.5 = (bf16[2,4,120,120]{3,2,1,0:T(8,128)(2,1)S(1)}, bf16[2,4,120,120]{3,2,1,0:T(8,128)(2,1)}, u32[]{:S(2)}) copy-start(bf16[2,4,120,120]{3,2,1,0:T(8,128)(2,1)} %taps_in.1) | copy-start | bytes 691204
  9.1 0.7 copy-start.7
  52.6 12.1 %copy-start.1 = (bf16[480,1024]{1,0:T(8,128)(2,1)S(1)}, bf16[480,1024]{1,0:T(8,128)(2,1)}, u32[]{:S(2)}) copy-start(bf16[480,1024]{1,0:T(8,128)(2,1)} %param.16) | copy-start | bytes 2949124
  52.6 30.0 %copy-start.6 = (s32[1,64,100]{2,1,0:T(8,128)S(1)}, s32[1,64,100]{2,1,0:T(8,128)}, u32[]{:S(2)}) copy-start(s32[1,64,100]{2,1,0:T(8,128)} %param.21) | copy-start | bytes 76804

commit v4 on v3

v4 whole, which is shorter than its diff:
```python
import functools

import jax
import jax.numpy as jnp
from jax import lax
from jax.experimental import pallas as pl
from jax.experimental.pallas import tpu as pltpu
from jax.sharding import PartitionSpec as P

KERNEL = 128
MASK_LEN = 10
SHIFTS = 16
LANES = 128


ln_eps = 1e-05
norm_eps = 1e-06
logit_temp = 0.1


def exact_gelu(value):
    return 0.5 * value * (1.0 + lax.erf(value * (0.5**0.5)))


def remote(src, dst, send, recv, **coords):
    return pltpu.make_async_remote_copy(
        src_ref=src,
        dst_ref=dst,
        send_sem=send,
        recv_sem=recv,
        device_id=coords,
        device_id_type=pl.DeviceIdType.MESH,
    )


def greet(barrier, **coords):
    pl.semaphore_signal(
        barrier, inc=1, device_id=coords, device_id_type=pl.DeviceIdType.MESH
    )


def frame_mask(starts, first, frames):
    position = first + lax.broadcasted_iota(jnp.int32, (frames, starts.shape[1]), 0)
    inside = (position >= starts) & (position < starts + MASK_LEN)
    return jnp.max(jnp.where(inside, 1.0, 0.0), axis=-1, keepdims=True)


def main_body(
    sizes,
    x_hbm,
    cw_hbm,
    pw_hbm,
    embed_hbm,
    starts_hbm,
    book_hbm,
    qw_hbm,
    fw_hbm,
    taps_in,
    codes_in,
    context_ref,
    targets_ref,
    norms_ref,
    x_in,
    cw_ref,
    pw_ref,
    embed_ref,
    starts_ref,
    book_ref,
    qw_ref,
    fw_ref,
    taps_ref,
    codes_ref,
    choice,
    codevec,
    x_wide,
    term_wide,
    term_half,
    arrived,
    feat,
    hidden,
    win_ref,
    xf,
    xc,
    wc,
    acc,
    mixed,
    gathered,
    part_half,
    part_arrived,
    load_sem,
    local_sem,
    code_send,
    code_recv,
    tap_send,
    tap_recv,
    ring_send,
    ring_recv,
    pair_send,
    pair_recv,
    sum_send,
    sum_recv,
    feat_send,
    feat_recv,
    win_send,
    win_recv,
    mix_send,
    mix_recv,
    part_send,
    part_recv,
):
    dps, seqs, tensors = sizes
    chips = seqs // 2
    dp, seq, tensor = (lax.axis_index(name) for name in ("dp", "seq", "tensor"))
    utts, frames, channels = term_wide.shape
    inner = taps_ref.shape[-1]

    def other_dp(k):
        return lax.rem(dp + k, dps)

    def other_seq(k):
        return lax.rem(seq + (k + seqs) % seqs, seqs)

    def other_tensor(k):
        return lax.rem(tensor + k, tensors)

    loads = [
        pltpu.make_async_copy(source, target, load_sem.at[index])
        for index, (source, target) in enumerate(
            (
                (x_hbm, x_in),
                (cw_hbm, cw_ref),
                (pw_hbm, pw_ref),
                (embed_hbm, embed_ref),
                (starts_hbm, starts_ref),
                (book_hbm, book_ref),
                (qw_hbm, qw_ref),
                (fw_hbm, fw_ref),
            )
        )
    ]
    for copy in loads:
        copy.start()
    local = pltpu.make_async_copy(taps_in.at[:, dp], taps_ref.at[dp, seq], local_sem.at[0])
    local.start()
    local_codes = pltpu.make_async_copy(codes_in, codes_ref.at[seq], local_sem.at[1])
    local_codes.start()

    barrier = pltpu.get_barrier_semaphore()
    for k in range(1, seqs):
        greet(barrier, seq=other_seq(k))
    for k in range(1, dps):
        for side in (-1, 0, 1):
            greet(barrier, dp=other_dp(k), seq=other_seq(side))
    for k in range(1, tensors):
        greet(barrier, tensor=other_tensor(k))
    pl.semaphore_wait(barrier, (seqs - 1) + 3 * (dps - 1) + (tensors - 1))

    pending = []

    def begin(copy):
        copy.start()
        pending.append(copy)
        return copy

    tap_copies = [
        begin(
            remote(
                taps_in.at[:, other_dp(k)],
                taps_ref.at[dp, seq],
                tap_send.at[k - 1],
                tap_recv.at[k - 1],
                dp=other_dp(k),
            )
        )
        for k in range(1, dps)
    ]
    code_copies = [
        begin(
            remote(
                codes_in,
                codes_ref.at[seq],
                code_send.at[k - 1],
                code_recv.at[k - 1],
                seq=other_seq(k),
            )
        )
        for k in range(1, seqs)
    ]

    loads[0].wait()
    loads[1].wait()
    x_wide[...] = x_in[...].reshape(x_wide.shape).astype(jnp.float32)
    term = jnp.zeros((utts * frames, channels), jnp.float32)
    for tap in range(2):
        rows = x_wide[pl.ds(tap, utts * frames, stride=2), :].astype(jnp.bfloat16)
        term += jnp.dot(rows, cw_ref[tap], preferred_element_type=jnp.float32)
    term = term.reshape(utts, frames, channels)
    term_wide[...] = term
    term_half[...] = term.astype(jnp.bfloat16)
    sum_copies = [
        begin(
            remote(
                term_half.at[other_tensor(k)],
                arrived.at[k - 1],
                sum_send.at[k - 1],
                sum_recv.at[k - 1],
                tensor=other_tensor(k),
            )
        )
        for k in range(1, tensors)
    ]

    local.wait()
    for copy in tap_copies:
        copy.wait_recv()

    core = lax.rem(seq, 2)
    sibling = seq + 1 - 2 * core
    ups, downs = chips // 2, (chips - 1) // 2
    split = dps // 2

    def block_of(hop, part):
        index = lax.rem(seq + 2 * hop + seqs, seqs)
        if part is None:
            return taps_ref.at[:, index]
        return taps_ref.at[pl.ds(part * split, split), index]

    def pass_block(slot, hop, part=None):
        block = block_of(hop, part)
        return begin(
            remote(block, block, pair_send.at[slot], pair_recv.at[slot], seq=sibling)
        )

    def ring(slot, hop, direction, part=None):
        block = block_of(hop, part)
        return begin(
            remote(
                block,
                block,
                ring_send.at[slot],
                ring_recv.at[slot],
                seq=other_seq(2 * direction),
            )
        )

    up = [ring(0, 0, 1)]
    down = [ring(ups, 0, -1)]
    passed = {0: [pass_block(0, 0)]}

    def advance(step):
        last = step == ups
        up[step - 1].wait_recv()
        if not last:
            up.append(ring(step, -step, 1, 0 if step == ups - 1 else None))
        down[step - 1].wait_recv()
        if not last:
            down.append(ring(ups + step, step, -1, 1 if step == ups - 1 else None))
        if last:
            passed[-step] = [pass_block(step, -step, 0), pass_block(ups + step, -step, 1)]
        else:
            passed[-step] = [pass_block(step, -step)]
            passed[step] = [pass_block(ups + step, step)]

    summed = term_wide[tensor]
    for k, copy in enumerate(sum_copies):
        copy.wait_recv()
        summed = summed + arrived[k].astype(jnp.float32)
    row_mean = jnp.mean(summed, axis=-1, keepdims=True)
    row_square = jnp.mean(summed * summed, axis=-1, keepdims=True)
    normed = (summed - row_mean) * lax.rsqrt(row_square - row_mean * row_mean + ln_eps)
    feat[tensor] = exact_gelu(normed).astype(jnp.bfloat16)
    feat_copies = [
        begin(
            remote(
                feat.at[tensor],
                feat.at[tensor],
                feat_send.at[k - 1],
                feat_recv.at[k - 1],
                tensor=other_tensor(k),
            )
        )
        for k in range(1, tensors)
    ]
    for copy in loads[2:]:
        copy.wait()
    is_masked = (
        jnp.concatenate(
            [frame_mask(starts_ref[u : u + 1], seq * frames, frames) for u in range(utts)], axis=0
        )
        > 0
    )
    for copy in feat_copies:
        copy.wait_recv()
    features = feat[...].reshape(utts * frames, channels)
    embed = embed_ref[...].astype(jnp.float32)
    hidden[...] = jnp.zeros_like(hidden)
    for group in range(dps):
        here = slice(group * inner, (group + 1) * inner)
        projected = lax.dot_general(
            features,
            pw_ref[here, :],
            (((1,), (1,)), ((), ())),
            preferred_element_type=jnp.float32,
        )
        chosen = jnp.where(is_masked, embed[:, here], projected)
        hidden[group, :, :, :inner] = chosen.astype(jnp.bfloat16).reshape(utts, frames, inner)
    mine = pl.ds(dp * utts, utts)
    win_copies = []
    for k in range(dps):
        for side in (-1, 0, 1):
            slot = 3 * k + side + 1
            if k == 0 and side == 0:
                continue
            win_copies.append(
                begin(
                    remote(
                        hidden.at[other_dp(k)],
                        win_ref.at[mine, 1 - side],
                        win_send.at[slot],
                        win_recv.at[slot],
                        dp=other_dp(k),
                        seq=other_seq(side),
                    )
                )
            )
    win_ref[mine, 1] = hidden[dp]
    advance(1)
    local_codes.wait()
    for copy in code_copies:
        copy.wait_recv()
    for block in range(seqs):
        choice[:, block * frames : (block + 1) * frames] = codes_ref[block]
    entries, width = book_ref.shape[1:]
    half = choice.shape[1] // 2

    def make_targets(part):
        here = slice(part * half, (part + 1) * half)
        for qgroup in range(book_ref.shape[0]):
            row = lax.broadcasted_iota(jnp.int32, (entries, half), 0)
            onehot = jnp.where(row == choice[qgroup : qgroup + 1, here], 1.0, 0.0)
            codevec[:, qgroup * width : (qgroup + 1) * width] = lax.dot_general(
                onehot.astype(jnp.bfloat16),
                book_ref[qgroup],
                (((0,), (0,)), ((), ())),
                preferred_element_type=jnp.float32,
            ).astype(jnp.bfloat16)
        made = jnp.dot(codevec[...], qw_ref[...], preferred_element_type=jnp.float32)
        made = made.astype(jnp.bfloat16)
        targets_ref[here, :] = made
        made = made.astype(jnp.float32)
        norm = jnp.sum(made * made, axis=-1, keepdims=True)
        norms_ref[:, here] = jnp.transpose(jnp.broadcast_to(norm, (half, LANES)))[:1]

    make_targets(0)
    advance(2)
    for copy in win_copies:
        copy.wait_recv()

    @pl.when(seq == 0)
    def low_edge():
        win_ref[:, 0] = jnp.zeros_like(win_ref[:, 0])

    @pl.when(seq == seqs - 1)
    def high_edge():
        win_ref[:, 2] = jnp.zeros_like(win_ref[:, 2])

    kept = xc.shape[1]
    acc[...] = jnp.zeros_like(acc)
    wc[...] = jnp.zeros_like(wc)

    @pl.loop(0, dps * utts)
    def shift_copies(u):
        xf[...] = win_ref[u].reshape(xf.shape).astype(jnp.float32)
        for j in range(SHIFTS):
            xc[u, :, j * LANES : (j + 1) * LANES] = xf[j : j + kept, :].astype(jnp.bfloat16)

    span = acc.shape[1]
    joint = 4
    run = wc.shape[1]

    def conv_block(hop):
        for copy in passed[hop]:
            copy.wait_recv()
        chip = lax.div(lax.rem(seq - core + 2 * hop + seqs, seqs), 2)
        lane = pl.multiple_of(lax.rem(chip, 4) * run, run)
        base = lax.div(chip, 4) * SHIFTS
        for pair in range(dps // 2):
            for side in range(2):
                for i in range(4):
                    wc[
                        pair, i * LANES : i * LANES + inner, side * LANES : side * LANES + inner
                    ] = taps_ref[2 * pair + side, 2 * chip + i // 2, i % 2]

        @pl.loop(0, dps * utts // joint)
        def multiply(chunk):
            here = pl.ds(chunk * joint, joint)
            total = acc[here]
            for pair in range(dps // 2):
                first = pl.multiple_of(base + 64 * pair, SHIFTS)
                window = xc[here, pl.ds(first, span), pl.ds(lane, run)]
                total += jnp.dot(
                    window.reshape(joint * span, run),
                    wc[pair],
                    preferred_element_type=jnp.float32,
                ).reshape(joint, span, 2 * LANES)
            acc[here] = total

    conv_block(0)
    conv_block(1)
    conv_block(-1)
    advance(3)
    conv_block(2)
    conv_block(-2)
    make_targets(1)
    conv_block(3)
    conv_block(-3)
    advance(4)
    conv_block(-4)

    @pl.loop(0, dps * utts)
    def mix(u):
        conv_out = acc[u, :frames, :LANES] + acc[u, span - frames :, LANES:]
        own = win_ref[u, 1].astype(jnp.float32)
        mixed[u] = (own + exact_gelu(conv_out)).astype(jnp.bfloat16)

    mix_copies = [
        begin(
            remote(
                mixed.at[pl.ds(other_dp(k) * utts, utts)],
                gathered.at[dp],
                mix_send.at[k - 1],
                mix_recv.at[k - 1],
                dp=other_dp(k),
            )
        )
        for k in range(1, dps)
    ]
    gathered[dp] = mixed[mine]
    for copy in mix_copies:
        copy.wait_recv()
    code_dim = fw_ref.shape[1]
    part_copies = []
    for k in range(tensors):
        there = other_tensor(k + 1)
        total = jnp.zeros((frames, code_dim), jnp.float32)
        for group in range(dps):
            rows = gathered[group, there][:, :inner]
            weights = fw_ref[group * inner : (group + 1) * inner, :]
            total += jnp.dot(rows, weights, preferred_element_type=jnp.float32)
        if k < tensors - 1:
            part_half[k] = total.astype(jnp.bfloat16)
            part_copies.append(
                begin(
                    remote(
                        part_half.at[k],
                        part_arrived.at[k],
                        part_send.at[k],
                        part_recv.at[k],
                        tensor=there,
                    )
                )
            )
    for k, copy in enumerate(part_copies):
        copy.wait_recv()
        total += part_arrived[k].astype(jnp.float32)
    context_ref[...] = total.astype(jnp.bfloat16)
    for copy in pending:
        copy.wait_send()


def main_stage(sizes, x, cw, pw, embed, starts, book, qw, fw, taps, codes):
    dps, seqs, tensors = sizes
    utts, frames = x.shape[0], x.shape[1] // 2
    channels = cw.shape[2]
    code_dim = fw.shape[1]
    per, _, inner, outer = taps.shape
    hops = seqs // 2
    span = frames + KERNEL // dps
    hbm = pl.BlockSpec(memory_space=pltpu.HBM)
    vmem = pl.BlockSpec(memory_space=pltpu.VMEM)
    dma = pltpu.SemaphoreType.DMA
    half = jnp.bfloat16

    def like(array):
        return pltpu.VMEM(array.shape, array.dtype)

    return pl.pallas_call(
        functools.partial(main_body, sizes),
        out_shape=(
            jax.ShapeDtypeStruct((frames, code_dim), half),
            jax.ShapeDtypeStruct((seqs * frames, code_dim), half),
            jax.ShapeDtypeStruct((1, seqs * frames), jnp.float32),
        ),
        in_specs=[hbm] * 10,
        out_specs=(vmem, vmem, vmem),
        scratch_shapes=[
            like(x),
            like(cw),
            like(pw),
            like(embed),
            like(starts),
            like(book),
            like(qw),
            like(fw),
            pltpu.VMEM((dps, seqs, per, inner, outer), half),
            pltpu.VMEM((seqs,) + codes.shape, codes.dtype),
            pltpu.VMEM((codes.shape[0], seqs * frames), codes.dtype),
            pltpu.VMEM((seqs * frames // 2, qw.shape[0]), half),
            pltpu.VMEM((2 * utts * frames, x.shape[2]), jnp.float32),
            pltpu.VMEM((utts, frames, channels), jnp.float32),
            pltpu.VMEM((utts, frames, channels), half),
            pltpu.VMEM((tensors - 1, frames, channels), half),
            pltpu.VMEM((utts, frames, channels), half),
            pltpu.VMEM((dps, utts, frames, LANES), half),
            pltpu.VMEM((utts * dps, 3, frames, LANES), half),
            pltpu.VMEM((3 * frames, LANES), jnp.float32),
            pltpu.VMEM((utts * dps, 3 * frames - SHIFTS, SHIFTS * LANES), half),
            pltpu.VMEM((dps // 2, 4 * LANES, 2 * LANES), half),
            pltpu.VMEM((utts * dps, span, 2 * LANES), jnp.float32),
            pltpu.VMEM((utts * dps, frames, LANES), half),
            pltpu.VMEM((dps, utts, frames, LANES), half),
            pltpu.VMEM((tensors - 1, frames, code_dim), half),
            pltpu.VMEM((tensors - 1, frames, code_dim), half),
            dma((8,)),
            dma((2,)),
            dma((seqs - 1,)),
            dma((seqs - 1,)),
            dma((dps - 1,)),
            dma((dps - 1,)),
            dma((hops,)),
            dma((hops,)),
            dma((hops + 1,)),
            dma((hops + 1,)),
            dma((tensors - 1,)),
            dma((tensors - 1,)),
            dma((tensors - 1,)),
            dma((tensors - 1,)),
            dma((3 * dps,)),
            dma((3 * dps,)),
            dma((dps - 1,)),
            dma((dps - 1,)),
            dma((tensors - 1,)),
            dma((tensors - 1,)),
        ],
        compiler_params=pltpu.CompilerParams(
            collective_id=0, has_side_effects=True, vmem_limit_bytes=44 * 2**20
        ),
    )(x, cw, pw, embed, starts, book, qw, fw, taps, codes)


def loss_body(c_ref, t_ref, tn_ref, ids_ref, starts_ref, o_ref, ids):
    context = c_ref[...]
    frames, negs = ids_ref.shape
    ids[...] = jnp.zeros_like(ids)
    ids[:, :negs] = ids_ref[...]
    first = pl.multiple_of(lax.axis_index("seq") * frames, frames)
    scores = lax.dot_general(
        context, t_ref[...], (((1,), (1,)), ((), ())), preferred_element_type=jnp.float32
    )
    wide = context.astype(jnp.float32)
    own = t_ref[pl.ds(first, frames), :].astype(jnp.float32)
    ctx_norm = jnp.sum(wide * wide, axis=-1, keepdims=True) + norm_eps
    own_norm = jnp.sum(own * own, axis=-1, keepdims=True) + norm_eps
    pos_dot = jnp.sum(wide * own, axis=-1, keepdims=True)
    positive = pos_dot * lax.rsqrt(ctx_norm * own_norm) / logit_temp
    logits = scores * lax.rsqrt(ctx_norm * (tn_ref[...] + norm_eps)) / logit_temp
    powers = jnp.exp(logits)
    chosen = ids[...]
    lane = chosen % LANES
    chunk = chosen // LANES
    picked = jnp.zeros((frames, LANES), jnp.float32)
    for c in range(powers.shape[1] // LANES):
        found = jnp.take_along_axis(
            powers[:, c * LANES : (c + 1) * LANES], lane, axis=1, mode="promise_in_bounds"
        )
        picked = jnp.where(chunk == c, found, picked)
    real = lax.broadcasted_iota(jnp.int32, picked.shape, 1) < negs
    negatives = jnp.sum(jnp.where(real, picked, 0.0), axis=-1, keepdims=True)
    loss = jnp.log(jnp.exp(positive) + negatives) - positive
    starts = starts_ref[pl.ds(lax.axis_index("tensor"), 1), :]
    o_ref[...] = jnp.where(frame_mask(starts, first, frames) > 0, loss, 0.0)


def losses(context, targets, norms, ids, starts):
    return pl.pallas_call(
        loss_body,
        out_shape=jax.ShapeDtypeStruct((ids.shape[0], 1), jnp.float32),
        scratch_shapes=[pltpu.VMEM((ids.shape[0], LANES), jnp.int32)],
        compiler_params=pltpu.CompilerParams(vmem_limit_bytes=24 * 2**20),
    )(context, targets, norms, ids, starts)


def on_device(
    feature_in,
    conv_weight,
    proj_weight,
    mask_embed,
    pos_weight,
    final_weight,
    codebook,
    quant_weight,
    mask_starts,
    code_choice,
    negative_ids,
):
    sizes = tuple(lax.axis_size(name) for name in ("dp", "seq", "tensor"))
    context, targets, norms = main_stage(
        sizes,
        feature_in,
        conv_weight,
        proj_weight.T,
        mask_embed.reshape(1, -1),
        mask_starts,
        codebook,
        quant_weight,
        final_weight,
        pos_weight,
        code_choice[0].T,
    )
    loss = losses(context, targets, norms, negative_ids[0], mask_starts)
    return loss.reshape(1, -1)


def solution(mesh):
    return jax.shard_map(
        on_device,
        mesh=mesh,
        in_specs=(
            P("dp", "seq", "tensor"),
            P(None, "tensor", None),
            P(None, "tensor"),
            P("tensor"),
            P(("dp", "seq"), "tensor", None, None),
            P("tensor", None),
            P(),
            P(),
            P("dp", None),
            P(("dp", "tensor"), "seq", None),
            P(("dp", "tensor"), "seq", None),
        ),
        out_specs=P(("dp", "tensor"), "seq"),
        check_vma=False,
    )
```

time: 84.5 us -> 78.1 us (0.924)
  Pallas kernels: 73.7 us -> 67.3 us
  local copies, waits for them, and re-layouts: 8.15 us -> 9.75 us
  other arithmetic: 2.22 us -> 0.63 us
    pallas_call x3 -> x1, Pallas kernels: 72.7 us -> 66.3 us  [main_stage(): pl.pallas_call(functools.partial(main_body, sizes), out_shape=(jax.ShapeD...]
    unnamed x16 -> x20, local copies, waits for them, and re-layouts: 6.29 us -> 9.07 us
    reshape x2 -> x1, local copies, waits for them, and re-layouts: 1.72 us -> 0.68 us  [on_device(): mask_embed.reshape(1, -1)]
    reduce_or x1 -> x0, other arithmetic: 0.9 us -> none  [on_device(): jnp.any((positions >= starts) & (positions < starts + MASK_LEN), axis=-1)]
where the time goes in v4:
time: 78.1 us; the launch traced here: 77.7 us
  Pallas kernels  67.3 us (86%)
  local copies, waits for them, and re-layouts  9.75 us (12%)
    pallas_call x1, Pallas kernels, main_stage(): pl.pallas_call(functools.partial(main_body, sizes), out_shape=(jax.ShapeD...  66.3 us
    unnamed x20, local copies, waits for them, and re-layouts  9.07 us

profile of v4, /device:TPU:1, one launch (start us, length us, event | category | flops | bytes accessed | tf_op | source)
XLA Modules:
  0.0 77.7 jit_solution(12686236919517693522)
XLA Ops:
  0.0 0.7 reshape.6.embed_hbm
  0.7 0.0 copy-start
  0.7 1.6 %copy-done = bf16[1024,1024]{1,0:T(8,128)(2,1)S(1)} copy-done((bf16[1024,1024]{1,0:T(8,128)(2,1)S(1)}, bf16[1024,1024]{1,0:T(8,128)(2,1)}, u32[]{:S(2)}) %copy-start) | copy-done | bytes 2097176
  2.3 0.0 copy-start.1
  2.3 1.2 %copy-done.1 = bf16[480,1024]{1,0:T(8,128)(2,1)S(1)} copy-done((bf16[480,1024]{1,0:T(8,128)(2,1)S(1)}, bf16[480,1024]{1,0:T(8,128)(2,1)}, u32[]{:S(2)}) %copy-start.1) | copy-done | bytes 983064
  3.5 0.0 copy-start.2
  3.5 1.1 %copy-done.2 = bf16[2,320,512]{2,1,0:T(8,128)(2,1)S(1)} copy-done((bf16[2,320,512]{2,1,0:T(8,128)(2,1)S(1)}, bf16[2,320,512]{2,1,0:T(8,128)(2,1)}, u32[]{:S(2)}) %copy-start.2) | copy-done | bytes 655384
  4.6 0.0 copy-start.3
  4.6 1.0 %copy-done.3 = bf16[512,480]{0,1:T(8,128)(2,1)S(1)} copy-done((bf16[512,480]{0,1:T(8,128)(2,1)S(1)}, bf16[512,480]{0,1:T(8,128)(2,1)}, u32[]{:S(2)}) %copy-start.3) | copy-done | bytes 491544
  5.6 0.0 copy-start.4
  5.6 0.9 %copy-done.4 = bf16[2,128,512]{2,1,0:T(8,128)(2,1)S(1)} copy-done((bf16[2,128,512]{2,1,0:T(8,128)(2,1)S(1)}, bf16[2,128,512]{2,1,0:T(8,128)(2,1)}, u32[]{:S(2)}) %copy-start.4) | copy-done | bytes 262168
  6.5 0.0 copy-start.5
  6.5 0.9 %copy-done.5 = bf16[2,4,120,120]{3,2,1,0:T(8,128)(2,1)S(1)} copy-done((bf16[2,4,120,120]{3,2,1,0:T(8,128)(2,1)S(1)}, bf16[2,4,120,120]{3,2,1,0:T(8,128)(2,1)}, u32[]{:S(2)}) %copy-start.5) | copy-done | bytes 230424
  7.5 0.0 copy-start.6
  7.5 0.9 %copy-done.6 = bf16[4,128,128]{2,1,0:T(8,128)(2,1)S(1)} copy-done((bf16[4,128,128]{2,1,0:T(8,128)(2,1)S(1)}, bf16[4,128,128]{2,1,0:T(8,128)(2,1)}, u32[]{:S(2)}) %copy-start.6) | copy-done | bytes 131096
  8.4 0.0 copy-start.8
  8.4 0.7 copy-done.8
  9.1 0.0 copy-start.9
  9.1 0.7 copy-done.9
  9.8 0.0 copy-start.7
  9.8 66.3 %shard_map.109 = (bf16[64,1024]{1,0:T(8,128)(2,1)S(1)}, bf16[1024,1024]{1,0:T(8,128)(2,1)S(1)}, f32[1,1024]{1,0:T(1,128)S(1)}) custom-call(bf16[4,128,128]{2,1,0:T(8,128)(2,1)S(1)} %copy-done.6, bf16[2,128,512]{2,1,0:T(8,128)(2,1)S(1)} %copy-done.4, bf16[480,512]{1,0:T(8,128)(2,1)S(1)} %bitcast.6, bf16[1,480]{1,0:T(2,128)(2,1)S(1)} %reshape.6.embed_hbm, ...), custom_call_target="tpu_custom_call" | custom-call | tf_op jit(solution)/shard_map/pallas_call | solution.py:487
  76.1 0.0 copy-done.7
  76.1 1.0 %shard_map.110 = f32[64,1]{1,0:T(8,128)S(1)} custom-call(bf16[64,1024]{1,0:T(8,128)(2,1)S(1)} %get-tuple-element.8.c_ref, bf16[1024,1024]{1,0:T(8,128)(2,1)S(1)} %get-tuple-element.9.t_ref, f32[1,1024]{1,0:T(1,128)S(1)} %get-tuple-element.10.tn_ref, s32[64,100]{1,0:T(8,128)S(1)} %bitcast.7, s32[4,66]{1,0:T(4,128)S(1)} %copy-done.8), custom_call_target="tpu_custom_call" | custom-call | tf_op jit(solution)/shard_map/pallas_call | solution.py:585
  77.1 0.6 reduce
Async XLA Ops:
  0.7 1.6 %copy-start = (bf16[1024,1024]{1,0:T(8,128)(2,1)S(1)}, bf16[1024,1024]{1,0:T(8,128)(2,1)}, u32[]{:S(2)}) copy-start(bf16[1024,1024]{1,0:T(8,128)(2,1)} %qw_hbm.1) | copy-start | bytes 6291460
  2.3 1.2 %copy-start.1 = (bf16[480,1024]{1,0:T(8,128)(2,1)S(1)}, bf16[480,1024]{1,0:T(8,128)(2,1)}, u32[]{:S(2)}) copy-start(bf16[480,1024]{1,0:T(8,128)(2,1)} %fw_hbm.1) | copy-start | bytes 2949124
  3.5 1.1 %copy-start.2 = (bf16[2,320,512]{2,1,0:T(8,128)(2,1)S(1)}, bf16[2,320,512]{2,1,0:T(8,128)(2,1)}, u32[]{:S(2)}) copy-start(bf16[2,320,512]{2,1,0:T(8,128)(2,1)} %book_hbm.1) | copy-start | bytes 1966084
  4.6 1.0 %copy-start.3 = (bf16[512,480]{0,1:T(8,128)(2,1)S(1)}, bf16[512,480]{0,1:T(8,128)(2,1)}, u32[]{:S(2)}) copy-start(bf16[512,480]{0,1:T(8,128)(2,1)} %param.13) | copy-start | bytes 1474564
  5.6 0.9 %copy-start.4 = (bf16[2,128,512]{2,1,0:T(8,128)(2,1)S(1)}, bf16[2,128,512]{2,1,0:T(8,128)(2,1)}, u32[]{:S(2)}) copy-start(bf16[2,128,512]{2,1,0:T(8,128)(2,1)} %cw_hbm.1) | copy-start | bytes 786436
  6.5 0.9 %copy-start.5 = (bf16[2,4,120,120]{3,2,1,0:T(8,128)(2,1)S(1)}, bf16[2,4,120,120]{3,2,1,0:T(8,128)(2,1)}, u32[]{:S(2)}) copy-start(bf16[2,4,120,120]{3,2,1,0:T(8,128)(2,1)} %taps_in.1) | copy-start | bytes 691204
  7.5 0.9 %copy-start.6 = (bf16[4,128,128]{2,1,0:T(8,128)(2,1)S(1)}, bf16[4,128,128]{2,1,0:T(8,128)(2,1)}, u32[]{:S(2)}) copy-start(bf16[4,128,128]{2,1,0:T(8,128)(2,1)} %x_hbm.1) | copy-start | bytes 393220
  8.4 0.7 copy-start.8
  9.1 0.7 copy-start.9
  9.8 66.3 %copy-start.7 = (s32[1,64,100]{2,1,0:T(8,128)S(1)}, s32[1,64,100]{2,1,0:T(8,128)}, u32[]{:S(2)}) copy-start(s32[1,64,100]{2,1,0:T(8,128)} %param.21) | copy-start | bytes 76804

commit v5 on v4

--- a/solution.py
+++ b/solution.py
@@ -57,7 +57,8 @@
     fw_hbm,
     taps_in,
     codes_in,
-    context_ref,
+    powers_ref,
+    positive_ref,
     targets_ref,
     norms_ref,
     x_in,
@@ -463,7 +464,22 @@
     for k, copy in enumerate(part_copies):
         copy.wait_recv()
         total += part_arrived[k].astype(jnp.float32)
-    context_ref[...] = total.astype(jnp.bfloat16)
+    context = total.astype(jnp.bfloat16)
+    scores = lax.dot_general(
+        context,
+        targets_ref[...],
+        (((1,), (1,)), ((), ())),
+        preferred_element_type=jnp.float32,
+    )
+    wide = context.astype(jnp.float32)
+    first = pl.multiple_of(seq * frames, frames)
+    own = targets_ref[pl.ds(first, frames), :].astype(jnp.float32)
+    ctx_norm = jnp.sum(wide * wide, axis=-1, keepdims=True) + norm_eps
+    own_norm = jnp.sum(own * own, axis=-1, keepdims=True) + norm_eps
+    pos_dot = jnp.sum(wide * own, axis=-1, keepdims=True)
+    positive_ref[...] = pos_dot * lax.rsqrt(ctx_norm * own_norm) / logit_temp
+    logits = scores * lax.rsqrt(ctx_norm * (norms_ref[...] + norm_eps)) / logit_temp
+    powers_ref[...] = jnp.exp(logits)
     for copy in pending:
         copy.wait_send()
 
@@ -487,13 +503,14 @@
     return pl.pallas_call(
         functools.partial(main_body, sizes),
         out_shape=(
-            jax.ShapeDtypeStruct((frames, code_dim), half),
-            jax.ShapeDtypeStruct((seqs * frames, code_dim), half),
-            jax.ShapeDtypeStruct((1, seqs * frames), jnp.float32),
+            jax.ShapeDtypeStruct((frames, seqs * frames), jnp.float32),
+            jax.ShapeDtypeStruct((frames, 1), jnp.float32),
         ),
         in_specs=[hbm] * 10,
-        out_specs=(vmem, vmem, vmem),
+        out_specs=(vmem, vmem),
         scratch_shapes=[
+            pltpu.VMEM((seqs * frames, code_dim), half),
+            pltpu.VMEM((1, seqs * frames), jnp.float32),
             like(x),
             like(cw),
             like(pw),
@@ -543,28 +560,17 @@
             dma((tensors - 1,)),
         ],
         compiler_params=pltpu.CompilerParams(
-            collective_id=0, has_side_effects=True, vmem_limit_bytes=44 * 2**20
+            collective_id=0, has_side_effects=True, vmem_limit_bytes=60 * 2**20
         ),
     )(x, cw, pw, embed, starts, book, qw, fw, taps, codes)
 
 
-def loss_body(c_ref, t_ref, tn_ref, ids_ref, starts_ref, o_ref, ids):
-    context = c_ref[...]
+def loss_body(powers_ref, positive_ref, ids_ref, starts_ref, o_ref, ids):
     frames, negs = ids_ref.shape
     ids[...] = jnp.zeros_like(ids)
     ids[:, :negs] = ids_ref[...]
-    first = pl.multiple_of(lax.axis_index("seq") * frames, frames)
-    scores = lax.dot_general(
-        context, t_ref[...], (((1,), (1,)), ((), ())), preferred_element_type=jnp.float32
-    )
-    wide = context.astype(jnp.float32)
-    own = t_ref[pl.ds(first, frames), :].astype(jnp.float32)
-    ctx_norm = jnp.sum(wide * wide, axis=-1, keepdims=True) + norm_eps
-    own_norm = jnp.sum(own * own, axis=-1, keepdims=True) + norm_eps
-    pos_dot = jnp.sum(wide * own, axis=-1, keepdims=True)
-    positive = pos_dot * lax.rsqrt(ctx_norm * own_norm) / logit_temp
-    logits = scores * lax.rsqrt(ctx_norm * (tn_ref[...] + norm_eps)) / logit_temp
-    powers = jnp.exp(logits)
+    powers = powers_ref[...]
+    positive = positive_ref[...]
     chosen = ids[...]
     lane = chosen % LANES
     chunk = chosen // LANES
@@ -578,16 +584,16 @@
     negatives = jnp.sum(jnp.where(real, picked, 0.0), axis=-1, keepdims=True)
     loss = jnp.log(jnp.exp(positive) + negatives) - positive
     starts = starts_ref[pl.ds(lax.axis_index("tensor"), 1), :]
-    o_ref[...] = jnp.where(frame_mask(starts, first, frames) > 0, loss, 0.0)
-
-
-def losses(context, targets, norms, ids, starts):
+    o_ref[...] = jnp.where(frame_mask(starts, lax.axis_index("seq") * frames, frames) > 0, loss, 0.0)
+
+
+def losses(powers, positive, ids, starts):
     return pl.pallas_call(
         loss_body,
         out_shape=jax.ShapeDtypeStruct((ids.shape[0], 1), jnp.float32),
         scratch_shapes=[pltpu.VMEM((ids.shape[0], LANES), jnp.int32)],
         compiler_params=pltpu.CompilerParams(vmem_limit_bytes=24 * 2**20),
-    )(context, targets, norms, ids, starts)
+    )(powers, positive, ids, starts)
 
 
 def on_device(
@@ -604,7 +610,7 @@
     negative_ids,
 ):
     sizes = tuple(lax.axis_size(name) for name in ("dp", "seq", "tensor"))
-    context, targets, norms = main_stage(
+    powers, positive = main_stage(
         sizes,
         feature_in,
         conv_weight,
@@ -617,7 +623,7 @@
         pos_weight,
         code_choice[0].T,
     )
-    loss = losses(context, targets, norms, negative_ids[0], mask_starts)
+    loss = losses(powers, positive, negative_ids[0], mask_starts)
     return loss.reshape(1, -1)
 
 

time: 78.1 us -> 71.3 us (0.913)
  local copies, waits for them, and re-layouts: 9.75 us -> 2.98 us
    unnamed x20 -> x8, local copies, waits for them, and re-layouts: 9.07 us -> 1.71 us
    pallas_call x1, Pallas kernels: 66.3 us -> 67.1 us  [main_stage(): pl.pallas_call(functools.partial(main_body, sizes), out_shape=(jax.ShapeD...]
where the time goes in v5:
time: 71.3 us; the launch traced here: 71.1 us
  Pallas kernels  67.5 us (95%)
  local copies, waits for them, and re-layouts  2.98 us (4%)
    pallas_call x1, Pallas kernels, main_stage(): pl.pallas_call(functools.partial(main_body, sizes), out_shape=(jax.ShapeD...  67.1 us
    unnamed x8, local copies, waits for them, and re-layouts  1.71 us

profile of v5, /device:TPU:1, one launch (start us, length us, event | category | flops | bytes accessed | tf_op | source)
XLA Modules:
  0.0 71.1 jit_solution(14039598848286692322)
XLA Ops:
  0.0 1.3 %reshape.6.embed_hbm = bf16[1,480]{1,0:T(2,128)(2,1)} reshape(bf16[480]{0:T(512)(128)(2,1)} %param.14) | data formatting | bytes 1920 | tf_op jit(solution)/shard_map/reshape | solution.py:618
  1.3 0.0 copy-start.1
  1.3 0.0 copy-start.3
  1.3 67.1 %shard_map.109 = (f32[64,1024]{1,0:T(8,128)}, f32[64,1]{1,0:T(8,128)}) custom-call(bf16[4,128,128]{2,1,0:T(8,128)(2,1)} %x_hbm.1, bf16[2,128,512]{2,1,0:T(8,128)(2,1)} %cw_hbm.1, bf16[480,512]{1,0:T(8,128)(2,1)} %bitcast.7, bf16[1,480]{1,0:T(2,128)(2,1)} %reshape.6.embed_hbm, s32[4,66]{1,0:T(4,128)} %starts_ref.1, bf16[2,320,512]{2,1,0:T(8,128)(2,1)} %book_hbm.1, ...), custom_call_target="tpu_custom_call" | custom-call | tf_op jit(solution)/shard_map/pallas_call | solution.py:503
  68.4 0.0 copy-done.1
  68.4 0.0 copy-done.3
  68.4 0.0 copy-start
  68.4 0.9 %copy-done = f32[64,1024]{1,0:T(8,128)S(1)} copy-done((f32[64,1024]{1,0:T(8,128)S(1)}, f32[64,1024]{1,0:T(8,128)}, u32[]{:S(2)}) %copy-start) | copy-done | bytes 262168
  69.4 0.0 copy-start.2
  69.4 0.8 %copy-done.2 = f32[64,1]{1,0:T(8,128)S(1)} copy-done((f32[64,1]{1,0:T(8,128)S(1)}, f32[64,1]{1,0:T(8,128)}, u32[]{:S(2)}) %copy-start.2) | copy-done | bytes 280
  70.1 0.3 shard_map.110
  70.5 0.6 reduce
Async XLA Ops:
  1.3 67.1 %copy-start.1 = (s32[1,64,100]{2,1,0:T(8,128)S(1)}, s32[1,64,100]{2,1,0:T(8,128)}, u32[]{:S(2)}) copy-start(s32[1,64,100]{2,1,0:T(8,128)} %param.21) | copy-start | bytes 76804
  1.3 67.1 %copy-start.3 = (s32[4,66]{1,0:T(4,128)S(1)}, s32[4,66]{1,0:T(4,128)}, u32[]{:S(2)}) copy-start(s32[4,66]{1,0:T(4,128)} %starts_ref.1) | copy-start | bytes 3172
  68.4 1.0 %copy-start = (f32[64,1024]{1,0:T(8,128)S(1)}, f32[64,1024]{1,0:T(8,128)}, u32[]{:S(2)}) copy-start(f32[64,1024]{1,0:T(8,128)} %get-tuple-element.7.powers_ref) | copy-start | bytes 786436
  69.4 0.8 %copy-start.2 = (f32[64,1]{1,0:T(8,128)S(1)}, f32[64,1]{1,0:T(8,128)}, u32[]{:S(2)}) copy-start(f32[64,1]{1,0:T(8,128)} %get-tuple-element.8.positive_ref) | copy-start | bytes 772

commit v6 on v5

--- a/solution.py
+++ b/solution.py
@@ -86,8 +86,7 @@
     acc,
     mixed,
     gathered,
-    part_half,
-    part_arrived,
+    joined,
     load_sem,
     local_sem,
     code_send,
@@ -106,8 +105,10 @@
     win_recv,
     mix_send,
     mix_recv,
-    part_send,
-    part_recv,
+    final_send,
+    final_recv,
+    side_send,
+    side_recv,
 ):
     dps, seqs, tensors = sizes
     chips = seqs // 2
@@ -135,7 +136,6 @@
                 (starts_hbm, starts_ref),
                 (book_hbm, book_ref),
                 (qw_hbm, qw_ref),
-                (fw_hbm, fw_ref),
             )
         )
     ]
@@ -145,6 +145,8 @@
     local.start()
     local_codes = pltpu.make_async_copy(codes_in, codes_ref.at[seq], local_sem.at[1])
     local_codes.start()
+    local_final = pltpu.make_async_copy(fw_hbm, fw_ref.at[tensor], local_sem.at[2])
+    local_final.start()
 
     barrier = pltpu.get_barrier_semaphore()
     for k in range(1, seqs):
@@ -153,8 +155,9 @@
         for side in (-1, 0, 1):
             greet(barrier, dp=other_dp(k), seq=other_seq(side))
     for k in range(1, tensors):
-        greet(barrier, tensor=other_tensor(k))
-    pl.semaphore_wait(barrier, (seqs - 1) + 3 * (dps - 1) + (tensors - 1))
+        for m in range(dps):
+            greet(barrier, tensor=other_tensor(k), dp=other_dp(m))
+    pl.semaphore_wait(barrier, (seqs - 1) + 3 * (dps - 1) + (tensors - 1) * dps)
 
     pending = []
 
@@ -277,6 +280,18 @@
                 feat.at[tensor],
                 feat_send.at[k - 1],
                 feat_recv.at[k - 1],
+                tensor=other_tensor(k),
+            )
+        )
+        for k in range(1, tensors)
+    ]
+    final_copies = [
+        begin(
+            remote(
+                fw_hbm.at[core],
+                fw_ref.at[tensor, core],
+                final_send.at[k - 1],
+                final_recv.at[k - 1],
                 tensor=other_tensor(k),
             )
         )
@@ -376,10 +391,9 @@
             xc[u, :, j * LANES : (j + 1) * LANES] = xf[j : j + kept, :].astype(jnp.bfloat16)
 
     span = acc.shape[1]
-    joint = 4
     run = wc.shape[1]
 
-    def conv_block(hop):
+    def load_block(hop):
         for copy in passed[hop]:
             copy.wait_recv()
         chip = lax.div(lax.rem(seq - core + 2 * hop + seqs, seqs), 2)
@@ -391,20 +405,27 @@
                     wc[
                         pair, i * LANES : i * LANES + inner, side * LANES : side * LANES + inner
                     ] = taps_ref[2 * pair + side, 2 * chip + i // 2, i % 2]
-
-        @pl.loop(0, dps * utts // joint)
+        return lane, base
+
+    def chunk_total(chunk, lane, base):
+        here = pl.ds(chunk * utts, utts)
+        total = acc[here]
+        for pair in range(dps // 2):
+            first = pl.multiple_of(base + 64 * pair, SHIFTS)
+            window = xc[here, pl.ds(first, span), pl.ds(lane, run)]
+            total += jnp.dot(
+                window.reshape(utts * span, run),
+                wc[pair],
+                preferred_element_type=jnp.float32,
+            ).reshape(utts, span, 2 * LANES)
+        return total
+
+    def conv_block(hop):
+        lane, base = load_block(hop)
+
+        @pl.loop(0, dps)
         def multiply(chunk):
-            here = pl.ds(chunk * joint, joint)
-            total = acc[here]
-            for pair in range(dps // 2):
-                first = pl.multiple_of(base + 64 * pair, SHIFTS)
-                window = xc[here, pl.ds(first, span), pl.ds(lane, run)]
-                total += jnp.dot(
-                    window.reshape(joint * span, run),
-                    wc[pair],
-                    preferred_element_type=jnp.float32,
-                ).reshape(joint, span, 2 * LANES)
-            acc[here] = total
+            acc[pl.ds(chunk * utts, utts)] = chunk_total(chunk, lane, base)
 
     conv_block(0)
     conv_block(1)
@@ -414,56 +435,52 @@
     conv_block(-2)
     make_targets(1)
     conv_block(3)
+    final_passes = []
+    for k, copy in enumerate(final_copies):
+        copy.wait_recv()
+        block = fw_ref.at[lax.rem(tensor + tensors - k - 1, tensors), core]
+        final_passes.append(
+            begin(remote(block, block, side_send.at[k], side_recv.at[k], seq=sibling))
+        )
+    advance(4)
     conv_block(-3)
-    advance(4)
-    conv_block(-4)
-
-    @pl.loop(0, dps * utts)
-    def mix(u):
-        conv_out = acc[u, :frames, :LANES] + acc[u, span - frames :, LANES:]
-        own = win_ref[u, 1].astype(jnp.float32)
-        mixed[u] = (own + exact_gelu(conv_out)).astype(jnp.bfloat16)
-
-    mix_copies = [
-        begin(
-            remote(
-                mixed.at[pl.ds(other_dp(k) * utts, utts)],
-                gathered.at[dp],
-                mix_send.at[k - 1],
-                mix_recv.at[k - 1],
-                dp=other_dp(k),
-            )
-        )
-        for k in range(1, dps)
-    ]
-    gathered[dp] = mixed[mine]
-    for copy in mix_copies:
-        copy.wait_recv()
-    code_dim = fw_ref.shape[1]
-    part_copies = []
-    for k in range(tensors):
-        there = other_tensor(k + 1)
-        total = jnp.zeros((frames, code_dim), jnp.float32)
-        for group in range(dps):
-            rows = gathered[group, there][:, :inner]
-            weights = fw_ref[group * inner : (group + 1) * inner, :]
-            total += jnp.dot(rows, weights, preferred_element_type=jnp.float32)
-        if k < tensors - 1:
-            part_half[k] = total.astype(jnp.bfloat16)
-            part_copies.append(
+
+    lane, base = load_block(-4)
+    mix_copies = []
+    for k in (1, 2, 3, 0):
+        chunk = other_dp(k)
+        total = chunk_total(chunk, lane, base)
+        conv_out = total[:, :frames, :LANES] + total[:, span - frames :, LANES:]
+        own = win_ref[pl.ds(chunk * utts, utts), 1].astype(jnp.float32)
+        mixed[pl.ds(chunk * utts, utts)] = (own + exact_gelu(conv_out)).astype(jnp.bfloat16)
+        for m in (2, 1, 3, 0):
+            if k == 0 and m == 0:
+                continue
+            slot = k * tensors + m
+            mix_copies.append(
                 begin(
                     remote(
-                        part_half.at[k],
-                        part_arrived.at[k],
-                        part_send.at[k],
-                        part_recv.at[k],
-                        tensor=there,
+                        mixed.at[chunk * utts + other_tensor(m)],
+                        gathered.at[tensor * dps + dp],
+                        mix_send.at[slot],
+                        mix_recv.at[slot],
+                        dp=chunk,
+                        tensor=other_tensor(m),
                     )
                 )
             )
-    for k, copy in enumerate(part_copies):
+    gathered[tensor * dps + dp] = mixed[dp * utts + tensor]
+    local_final.wait()
+    for copy in final_passes + mix_copies:
         copy.wait_recv()
-        total += part_arrived[k].astype(jnp.float32)
+    code_dim = fw_ref.shape[-1]
+    for group in range(tensors * dps):
+        joined[:, group * inner : (group + 1) * inner] = gathered[group][:, :inner]
+    total = jnp.dot(
+        joined[...],
+        fw_ref[...].reshape(joined.shape[1], code_dim),
+        preferred_element_type=jnp.float32,
+    )
     context = total.astype(jnp.bfloat16)
     scores = lax.dot_general(
         context,
@@ -488,7 +505,7 @@
     dps, seqs, tensors = sizes
     utts, frames = x.shape[0], x.shape[1] // 2
     channels = cw.shape[2]
-    code_dim = fw.shape[1]
+    code_dim = fw.shape[2]
     per, _, inner, outer = taps.shape
     hops = seqs // 2
     span = frames + KERNEL // dps
@@ -518,7 +535,7 @@
             like(starts),
             like(book),
             like(qw),
-            like(fw),
+            pltpu.VMEM((tensors,) + fw.shape, half),
             pltpu.VMEM((dps, seqs, per, inner, outer), half),
             pltpu.VMEM((seqs,) + codes.shape, codes.dtype),
             pltpu.VMEM((codes.shape[0], seqs * frames), codes.dtype),
@@ -535,11 +552,10 @@
             pltpu.VMEM((dps // 2, 4 * LANES, 2 * LANES), half),
             pltpu.VMEM((utts * dps, span, 2 * LANES), jnp.float32),
             pltpu.VMEM((utts * dps, frames, LANES), half),
-            pltpu.VMEM((dps, utts, frames, LANES), half),
-            pltpu.VMEM((tensors - 1, frames, code_dim), half),
-            pltpu.VMEM((tensors - 1, frames, code_dim), half),
-            dma((8,)),
-            dma((2,)),
+            pltpu.VMEM((tensors * dps, frames, LANES), half),
+            pltpu.VMEM((frames, tensors * dps * inner), half),
+            dma((7,)),
+            dma((3,)),
             dma((seqs - 1,)),
             dma((seqs - 1,)),
             dma((dps - 1,)),
@@ -554,8 +570,10 @@
             dma((tensors - 1,)),
             dma((3 * dps,)),
             dma((3 * dps,)),
-            dma((dps - 1,)),
-            dma((dps - 1,)),
+            dma((dps * tensors,)),
+            dma((dps * tensors,)),
+            dma((tensors - 1,)),
+            dma((tensors - 1,)),
             dma((tensors - 1,)),
             dma((tensors - 1,)),
         ],
@@ -619,7 +637,7 @@
         mask_starts,
         codebook,
         quant_weight,
-        final_weight,
+        final_weight.reshape(2, -1, final_weight.shape[1]),
         pos_weight,
         code_choice[0].T,
     )

time: 71.3 us -> 72.3 us (1.014)
  Pallas kernels: 67.5 us -> 68.5 us
    pallas_call x1, Pallas kernels: 67.1 us -> 68.1 us  [main_stage(): pl.pallas_call(functools.partial(main_body, sizes), out_shape=(jax.ShapeD...]
where the time goes in v6:
time: 72.3 us; the launch traced here: 72.1 us
  Pallas kernels  68.5 us (95%)
  local copies, waits for them, and re-layouts  2.98 us (4%)
    pallas_call x1, Pallas kernels, main_stage(): pl.pallas_call(functools.partial(main_body, sizes), out_shape=(jax.ShapeD...  68.1 us
    unnamed x8, local copies, waits for them, and re-layouts  1.71 us

profile of v6, /device:TPU:1, one launch (start us, length us, event | category | flops | bytes accessed | tf_op | source)
XLA Modules:
  0.0 72.1 jit_solution(15193677899367049372)
XLA Ops:
  0.0 1.3 %reshape.9.embed_hbm = bf16[1,480]{1,0:T(2,128)(2,1)} reshape(bf16[480]{0:T(512)(128)(2,1)} %param.14) | data formatting | bytes 1920 | tf_op jit(solution)/shard_map/reshape | solution.py:636
  1.3 0.0 copy-start.1
  1.3 0.0 copy-start.3
  1.3 68.1 %shard_map.109 = (f32[64,1024]{1,0:T(8,128)}, f32[64,1]{1,0:T(8,128)}) custom-call(bf16[4,128,128]{2,1,0:T(8,128)(2,1)} %x_hbm.1, bf16[2,128,512]{2,1,0:T(8,128)(2,1)} %cw_hbm.1, bf16[480,512]{1,0:T(8,128)(2,1)} %bitcast.9, bf16[1,480]{1,0:T(2,128)(2,1)} %reshape.9.embed_hbm, s32[4,66]{1,0:T(4,128)} %starts_ref.1, bf16[2,320,512]{2,1,0:T(8,128)(2,1)} %book_hbm.1, ...), custom_call_target="tpu_custom_call" | custom-call | tf_op jit(solution)/shard_map/pallas_call | solution.py:520
  69.4 0.0 copy-done.1
  69.4 0.0 copy-done.3
  69.5 0.0 copy-start
  69.5 0.9 %copy-done = f32[64,1024]{1,0:T(8,128)S(1)} copy-done((f32[64,1024]{1,0:T(8,128)S(1)}, f32[64,1024]{1,0:T(8,128)}, u32[]{:S(2)}) %copy-start) | copy-done | bytes 262168
  70.4 0.0 copy-start.2
  70.4 0.8 %copy-done.2 = f32[64,1]{1,0:T(8,128)S(1)} copy-done((f32[64,1]{1,0:T(8,128)S(1)}, f32[64,1]{1,0:T(8,128)}, u32[]{:S(2)}) %copy-start.2) | copy-done | bytes 280
  71.2 0.3 shard_map.110
  71.5 0.6 reduce
Async XLA Ops:
  1.3 68.2 %copy-start.1 = (s32[1,64,100]{2,1,0:T(8,128)S(1)}, s32[1,64,100]{2,1,0:T(8,128)}, u32[]{:S(2)}) copy-start(s32[1,64,100]{2,1,0:T(8,128)} %param.21) | copy-start | bytes 76804
  1.3 68.2 %copy-start.3 = (s32[4,66]{1,0:T(4,128)S(1)}, s32[4,66]{1,0:T(4,128)}, u32[]{:S(2)}) copy-start(s32[4,66]{1,0:T(4,128)} %starts_ref.1) | copy-start | bytes 3172
  69.5 1.0 %copy-start = (f32[64,1024]{1,0:T(8,128)S(1)}, f32[64,1024]{1,0:T(8,128)}, u32[]{:S(2)}) copy-start(f32[64,1024]{1,0:T(8,128)} %get-tuple-element.7.powers_ref) | copy-start | bytes 786436
  70.4 0.8 %copy-start.2 = (f32[64,1]{1,0:T(8,128)S(1)}, f32[64,1]{1,0:T(8,128)}, u32[]{:S(2)}) copy-start(f32[64,1]{1,0:T(8,128)} %get-tuple-element.8.positive_ref) | copy-start | bytes 772

commit v7 on v6

--- a/solution.py
+++ b/solution.py
@@ -265,6 +265,35 @@
             passed[-step] = [pass_block(step, -step)]
             passed[step] = [pass_block(ups + step, step)]
 
+    for copy in loads[2:]:
+        copy.wait()
+    local_codes.wait()
+    for copy in code_copies:
+        copy.wait_recv()
+    for block in range(seqs):
+        choice[:, block * frames : (block + 1) * frames] = codes_ref[block]
+    entries, width = book_ref.shape[1:]
+    half = choice.shape[1] // 2
+
+    def make_targets(part):
+        here = slice(part * half, (part + 1) * half)
+        for qgroup in range(book_ref.shape[0]):
+            row = lax.broadcasted_iota(jnp.int32, (entries, half), 0)
+            onehot = jnp.where(row == choice[qgroup : qgroup + 1, here], 1.0, 0.0)
+            codevec[:, qgroup * width : (qgroup + 1) * width] = lax.dot_general(
+                onehot.astype(jnp.bfloat16),
+                book_ref[qgroup],
+                (((0,), (0,)), ((), ())),
+                preferred_element_type=jnp.float32,
+            ).astype(jnp.bfloat16)
+        made = jnp.dot(codevec[...], qw_ref[...], preferred_element_type=jnp.float32)
+        made = made.astype(jnp.bfloat16)
+        targets_ref[here, :] = made
+        made = made.astype(jnp.float32)
+        norm = jnp.sum(made * made, axis=-1, keepdims=True)
+        norms_ref[:, here] = jnp.transpose(jnp.broadcast_to(norm, (half, LANES)))[:1]
+
+    make_targets(0)
     summed = term_wide[tensor]
     for k, copy in enumerate(sum_copies):
         copy.wait_recv()
@@ -297,8 +326,8 @@
         )
         for k in range(1, tensors)
     ]
-    for copy in loads[2:]:
-        copy.wait()
+    make_targets(1)
+    advance(1)
     is_masked = (
         jnp.concatenate(
             [frame_mask(starts_ref[u : u + 1], seq * frames, frames) for u in range(utts)], axis=0
@@ -340,34 +369,6 @@
                 )
             )
     win_ref[mine, 1] = hidden[dp]
-    advance(1)
-    local_codes.wait()
-    for copy in code_copies:
-        copy.wait_recv()
-    for block in range(seqs):
-        choice[:, block * frames : (block + 1) * frames] = codes_ref[block]
-    entries, width = book_ref.shape[1:]
-    half = choice.shape[1] // 2
-
-    def make_targets(part):
-        here = slice(part * half, (part + 1) * half)
-        for qgroup in range(book_ref.shape[0]):
-            row = lax.broadcasted_iota(jnp.int32, (entries, half), 0)
-            onehot = jnp.where(row == choice[qgroup : qgroup + 1, here], 1.0, 0.0)
-            codevec[:, qgroup * width : (qgroup + 1) * width] = lax.dot_general(
-                onehot.astype(jnp.bfloat16),
-                book_ref[qgroup],
-                (((0,), (0,)), ((), ())),
-                preferred_element_type=jnp.float32,
-            ).astype(jnp.bfloat16)
-        made = jnp.dot(codevec[...], qw_ref[...], preferred_element_type=jnp.float32)
-        made = made.astype(jnp.bfloat16)
-        targets_ref[here, :] = made
-        made = made.astype(jnp.float32)
-        norm = jnp.sum(made * made, axis=-1, keepdims=True)
-        norms_ref[:, here] = jnp.transpose(jnp.broadcast_to(norm, (half, LANES)))[:1]
-
-    make_targets(0)
     advance(2)
     for copy in win_copies:
         copy.wait_recv()
@@ -428,13 +429,12 @@
             acc[pl.ds(chunk * utts, utts)] = chunk_total(chunk, lane, base)
 
     conv_block(0)
+    advance(3)
     conv_block(1)
     conv_block(-1)
-    advance(3)
     conv_block(2)
     conv_block(-2)
-    make_targets(1)
-    conv_block(3)
+    advance(4)
     final_passes = []
     for k, copy in enumerate(final_copies):
         copy.wait_recv()
@@ -442,7 +442,7 @@
         final_passes.append(
             begin(remote(block, block, side_send.at[k], side_recv.at[k], seq=sibling))
         )
-    advance(4)
+    conv_block(3)
     conv_block(-3)
 
     lane, base = load_block(-4)

time: 72.3 us -> 70.8 us (0.979)
  Pallas kernels: 68.5 us -> 67 us
    pallas_call x1, Pallas kernels: 68.1 us -> 66.6 us  [main_stage(): pl.pallas_call(functools.partial(main_body, sizes), out_shape=(jax.ShapeD...]
where the time goes in v7:
time: 70.8 us; the launch traced here: 70.6 us
  Pallas kernels  67 us (95%)
  local copies, waits for them, and re-layouts  2.98 us (4%)
    pallas_call x1, Pallas kernels, main_stage(): pl.pallas_call(functools.partial(main_body, sizes), out_shape=(jax.ShapeD...  66.6 us
    unnamed x8, local copies, waits for them, and re-layouts  1.71 us

profile of v7, /device:TPU:1, one launch (start us, length us, event | category | flops | bytes accessed | tf_op | source)
XLA Modules:
  0.0 70.6 jit_solution(3105230665696787767)
XLA Ops:
  0.0 1.3 %reshape.9.embed_hbm = bf16[1,480]{1,0:T(2,128)(2,1)} reshape(bf16[480]{0:T(512)(128)(2,1)} %param.14) | data formatting | bytes 1920 | tf_op jit(solution)/shard_map/reshape | solution.py:636
  1.3 0.0 copy-start.1
  1.3 0.0 copy-start.3
  1.3 66.6 %shard_map.109 = (f32[64,1024]{1,0:T(8,128)}, f32[64,1]{1,0:T(8,128)}) custom-call(bf16[4,128,128]{2,1,0:T(8,128)(2,1)} %x_hbm.1, bf16[2,128,512]{2,1,0:T(8,128)(2,1)} %cw_hbm.1, bf16[480,512]{1,0:T(8,128)(2,1)} %bitcast.9, bf16[1,480]{1,0:T(2,128)(2,1)} %reshape.9.embed_hbm, s32[4,66]{1,0:T(4,128)} %starts_ref.1, bf16[2,320,512]{2,1,0:T(8,128)(2,1)} %book_hbm.1, ...), custom_call_target="tpu_custom_call" | custom-call | tf_op jit(solution)/shard_map/pallas_call | solution.py:520
  67.9 0.0 copy-done.1
  67.9 0.0 copy-done.3
  67.9 0.0 copy-start
  67.9 0.9 %copy-done = f32[64,1024]{1,0:T(8,128)S(1)} copy-done((f32[64,1024]{1,0:T(8,128)S(1)}, f32[64,1024]{1,0:T(8,128)}, u32[]{:S(2)}) %copy-start) | copy-done | bytes 262168
  68.9 0.0 copy-start.2
  68.9 0.8 %copy-done.2 = f32[64,1]{1,0:T(8,128)S(1)} copy-done((f32[64,1]{1,0:T(8,128)S(1)}, f32[64,1]{1,0:T(8,128)}, u32[]{:S(2)}) %copy-start.2) | copy-done | bytes 280
  69.6 0.3 shard_map.110
  70.0 0.6 reduce
Async XLA Ops:
  1.3 66.6 %copy-start.1 = (s32[1,64,100]{2,1,0:T(8,128)S(1)}, s32[1,64,100]{2,1,0:T(8,128)}, u32[]{:S(2)}) copy-start(s32[1,64,100]{2,1,0:T(8,128)} %param.21) | copy-start | bytes 76804
  1.3 66.6 %copy-start.3 = (s32[4,66]{1,0:T(4,128)S(1)}, s32[4,66]{1,0:T(4,128)}, u32[]{:S(2)}) copy-start(s32[4,66]{1,0:T(4,128)} %starts_ref.1) | copy-start | bytes 3172
  67.9 1.0 %copy-start = (f32[64,1024]{1,0:T(8,128)S(1)}, f32[64,1024]{1,0:T(8,128)}, u32[]{:S(2)}) copy-start(f32[64,1024]{1,0:T(8,128)} %get-tuple-element.7.powers_ref) | copy-start | bytes 786436
  68.9 0.8 %copy-start.2 = (f32[64,1]{1,0:T(8,128)S(1)}, f32[64,1]{1,0:T(8,128)}, u32[]{:S(2)}) copy-start(f32[64,1]{1,0:T(8,128)} %get-tuple-element.8.positive_ref) | copy-start | bytes 772
